TPU v7x, 256 devices: a whole 4x4x8 slice. The times are simulated.
256 devices in a mesh: rows: 128 (over y, z, x), blk: 2 (over core).
Axes of the slice: x: 4, y: 4, z: 8, core: 2. Of those that a mesh axis runs over, the one named last changes fastest.
Arguments:
- inputs: bfloat16 [131072, 440], P('rows'), may hold values from -6 to 6
- proj: bfloat16 [4, 440, 512], P('blk'), may hold values from -0.25 to 0.25
- phase: bfloat16 [4, 512], P('blk'), may hold values from -3.140625 to 3.140625
- targets: bfloat16 [131072, 1024], P('rows', 'blk'), may hold values from -6 to 6
Outputs:
- coefs: float32 [4, 512, 1024], P(None, None, 'blk')
- residual: float32 [131072, 1024], P('rows', 'blk')
All inputs are finite; a program needn't handle non-finite values.
Results may differ from a plain program's by a relative error of at most 0.0035.
The roundings to bfloat16 on the way count: a program that leaves them out, or rounds other values in their place, can miss the bound.
Values may be sent and summed in bfloat16 or wider, within the bound.
A program may use at most 128 MiB of HBM per device.

v0:
```python
import math

import jax
import jax.numpy as jnp
from jax import lax
from jax.sharding import PartitionSpec as P

ridge = 0.05


def broadcast(value, axis, root):
    mine = lax.axis_index(axis) == root
    return lax.psum(jnp.where(mine, value, jnp.zeros_like(value)), axis)


def build(inputs, weights, shift, factor_scale):
    pre = jnp.dot(inputs, weights, preferred_element_type=jnp.float32) + shift.astype(jnp.float32)
    return (jnp.cos(pre) * factor_scale).astype(jnp.bfloat16)


def body(inputs, proj, phase, targets):
    local_rows = inputs.shape[0]
    factor_scale = 1.0 / math.sqrt(local_rows * lax.axis_size("rows"))
    owned = proj.shape[0]
    width = proj.shape[2]
    feat_list = [build(inputs, proj[index], phase[index], factor_scale) for index in range(owned)]
    gram_list = [
        lax.dot_general(feats, feats, (((0,), (0,)), ((), ())), preferred_element_type=jnp.float32)
        for feats in feat_list
    ]
    summed = lax.psum(tuple(gram_list), "rows")
    identity_mat = jnp.eye(width, dtype=jnp.float32)
    own_factors = jnp.stack([jnp.linalg.cholesky(gram + ridge * identity_mat) for gram in summed])
    factors = lax.all_gather(own_factors, "blk", axis=0, tiled=True)
    total_blocks = owned * lax.axis_size("blk")
    residual = targets.astype(jnp.float32)
    coef_list = []
    for block in range(total_blocks):
        owner = block // owned
        local = block % owned
        feats = broadcast(feat_list[local], "blk", owner)
        partial_corr = lax.dot_general(
            feats,
            residual.astype(jnp.bfloat16),
            (((0,), (0,)), ((), ())),
            preferred_element_type=jnp.float32,
        )
        factor = factors[block]
        corr = lax.psum(partial_corr, "rows")
        delta = jax.scipy.linalg.cho_solve((factor, True), corr)
        coef_list.append(delta)
        residual = residual - jnp.dot(
            feats, delta.astype(jnp.bfloat16), preferred_element_type=jnp.float32
        )
    return (jnp.stack(coef_list), residual)


def solution(mesh):
    return jax.shard_map(
        body,
        mesh=mesh,
        in_specs=(P("rows", None), P("blk", None, None), P("blk", None), P("rows", "blk")),
        out_specs=(P(None, None, "blk"), P("rows", "blk")),
        check_vma=False,
    )
```

profile of v0, /device:TPU:1, one launch (start us, length us, event | category | flops | bytes accessed | tf_op | source)
XLA Modules:
  0.0 1289.7 jit_solution(14516420596076064928)
XLA Ops:
  8.4 9.9 broadcast_select_fusion.1
  31.5 40.5 %all-reduce.17.cloned.1.call-done = (bf16[1024,512]{1,0:T(8,128)(2,1)}, bf16[1024,512]{1,0:T(8,128)(2,1)}, bf16[1024,512]{1,0:T(8,128)(2,1)}, bf16[1024,512]{1,0:T(8,128)(2,1)}) async-done(((bf16[1024,512]{1,0:T(8,128)(2,1)}, bf16[1024,512]{1,0:T(8,128)(2,1)}, bf16[1024,512]{1,0:T(8,128)(2,1)}, bf16[1024,512]{1,0:T(8,128)(2,1)}), (bf16[1024,512]{1,0:T(8,128)(2,1)}, bf16[1024,512]{1,0:T(8,128)(2,1)}, ...) | async-done | bytes 4194320 | tf_op jit(solution)/shard_map/psum | solution.py:13
  75.1 233.0 %all-reduce.15.cloned.1.call-done = (f32[512,512]{1,0:T(8,128)}, f32[512,512]{0,1:T(8,128)}, f32[512,512]{0,1:T(8,128)}) async-done(((f32[512,512]{1,0:T(8,128)}, f32[512,512]{0,1:T(8,128)}, f32[512,512]{0,1:T(8,128)}), (f32[512,512]{1,0:T(8,128)}, f32[512,512]{0,1:T(8,128)}, f32[512,512]{0,1:T(8,128)})) %all-reduce.15.cloned.1.call-update) | async-done | bytes 3145744 | tf_op jit(solution)/shard_map/psum | solution.py:49
  314.0 11.7 cholesky.286
  338.2 11.7 cholesky.305
  351.3 10.0 custom-call.32
  362.9 11.7 cholesky.326
  386.6 12.1 cholesky.343
  403.4 11.7 cholesky.358
  415.1 9.8 custom-call.34
  427.6 11.7 cholesky.377
  440.6 9.9 custom-call.35
  452.2 11.7 cholesky.398
  475.8 11.7 cholesky.415
  496.2 21.8 %all-gather.2.cloned.1.call-done = f32[4,512,512]{2,1,0:T(8,128)} async-done(((f32[2,512,512]{2,1,0:T(8,128)}), f32[4,512,512]{2,1,0:T(8,128)}) %all-gather.2.cloned.1.call-update) | async-done | bytes 4194320 | tf_op jit(solution)/shard_map/all_gather | solution.py:34
  530.2 39.3 %custom-call.37 = f32[4,128,128]{1,2,0:T(8,128)S(1)} custom-call(f32[4,128,128]{2,1,0:T(8,128)S(1)} %get-tuple-element.30), custom_call_target="InvertDiagBlocksLowerTriangular" | custom-call | tf_op jit(solution)/shard_map/jit(_cho_solve)/triangular_solve | solution.py:50
  579.4 11.9 while.9
  591.3 39.3 %custom-call.38 = f32[4,128,128]{1,2,0:T(8,128)S(1)} custom-call(f32[4,128,128]{2,1,0:T(8,128)S(1)} %get-tuple-element.31), custom_call_target="InvertDiagBlocksLowerTriangular" | custom-call | tf_op jit(solution)/shard_map/jit(_cho_solve)/triangular_solve | solution.py:50
  630.6 168.0 %all-reduce.9.cloned.1.call-done = f32[512,512]{1,0:T(8,128)} async-done(((f32[512,512]{1,0:T(8,128)}), f32[512,512]{1,0:T(8,128)}) %all-reduce.9.cloned.1.call-update) | async-done | bytes 1048592 | tf_op jit(solution)/shard_map/psum | solution.py:49
  820.6 39.3 %custom-call.39 = f32[4,128,128]{1,2,0:T(8,128)S(1)} custom-call(f32[4,128,128]{2,1,0:T(8,128)S(1)} %get-tuple-element.32), custom_call_target="InvertDiagBlocksLowerTriangular" | custom-call | tf_op jit(solution)/shard_map/jit(_cho_solve)/triangular_solve | solution.py:50
  859.9 173.9 %all-reduce.11.cloned.1.call-done = f32[512,512]{1,0:T(8,128)} async-done(((f32[512,512]{1,0:T(8,128)}), f32[512,512]{1,0:T(8,128)}) %all-reduce.11.cloned.1.call-update) | async-done | bytes 1048592 | tf_op jit(solution)/shard_map/psum | solution.py:49
  1046.0 14.3 %while.11 = (s32[]{:T(128)}, f32[512,512]{1,0:T(8,128)}, s32[4,2]{0,1:T(2,128)S(1)}, f32[4,128,128]{2,1,0:T(8,128)}, s32[]{:T(128)}) while((s32[]{:T(128)}, f32[512,512]{1,0:T(8,128)}, s32[4,2]{0,1:T(2,128)S(1)}, f32[4,128,128]{2,1,0:T(8,128)}, s32[]{:T(128)}) %tuple.120), condition=%wide.while_cond.clone.2, body=%wide.while_body.clone.2.sunk | while | flops 2 | bytes 132705 | solution.py:50
  1060.3 40.9 %custom-call.40 = f32[4,128,128]{1,2,0:T(8,128)} custom-call(f32[4,128,128]{2,1,0:T(8,128)} %get-tuple-element.33), custom_call_target="InvertDiagBlocksLowerTriangular" | custom-call | tf_op jit(solution)/shard_map/jit(_cho_solve)/triangular_solve | solution.py:50
  1105.5 160.7 %all-reduce.13.cloned.1.call-done = f32[512,512]{1,0:T(8,128)} async-done(((f32[512,512]{1,0:T(8,128)}), f32[512,512]{1,0:T(8,128)}) %all-reduce.13.cloned.1.call-update) | async-done | bytes 1048592 | tf_op jit(solution)/shard_map/psum | solution.py:49
  (269 shorter events, 194.3 us)
Async XLA Ops:
  7.2 64.7 %all-reduce.17.cloned.1.call-start = ((), (), s32[]{:S(2)}) async-start(), calls=%async_computation.5 | async-start | bytes 8388608 | tf_op jit(solution)/shard_map/psum | solution.py:13
  8.4 9.9 copy-start.39
  27.9 280.1 %all-reduce.15.cloned.1.call-start = ((), (), s32[]{:S(2)}) async-start(), calls=%async_computation.4 | async-start | bytes 6291456 | tf_op jit(solution)/shard_map/psum | solution.py:49
  29.7 42.2 %copy-start.32 = (bf16[1024,512]{1,0:T(8,128)(2,1)S(1)}, bf16[1024,512]{1,0:T(8,128)(2,1)}, u32[]{:S(2)}) copy-start(bf16[1024,512]{1,0:T(8,128)(2,1)} %param.10) | copy-start | bytes 3145732
  74.9 443.1 %all-gather.2.cloned.1.call-start = ((), (), s32[]{:S(2)}) async-start(), calls=%async_computation | async-start | bytes 6291456 | tf_op jit(solution)/shard_map/all_gather | solution.py:34
  491.9 2.6 copy-start.10
  496.1 302.4 %all-reduce.9.cloned.1.call-start = ((), (), s32[]{:S(2)}) async-start(), calls=%async_computation.1 | async-start | bytes 2097152 | tf_op jit(solution)/shard_map/psum | solution.py:49
  496.2 73.3 %copy-start.37 = (f32[512,512]{1,0:T(8,128)S(1)}, f32[512,512]{1,0:T(8,128)}, u32[]{:S(2)}) copy-start(f32[512,512]{1,0:T(8,128)} %get-tuple-element.66) | copy-start | bytes 3145732
  573.5 2.3 copy-start.33
  573.5 2.3 copy-start.34
  578.9 454.9 %all-reduce.11.cloned.1.call-start = ((), (), s32[]{:S(2)}) async-start(), calls=%async_computation.2 | async-start | bytes 2097152 | tf_op jit(solution)/shard_map/psum | solution.py:49
  798.5 3.3 copy-start.8
  812.7 453.6 %all-reduce.13.cloned.1.call-start = ((), (), s32[]{:S(2)}) async-start(), calls=%async_computation.3 | async-start | bytes 2097152 | tf_op jit(solution)/shard_map/psum | solution.py:49
  1033.8 3.2 copy-start.38
  1039.8 2.3 copy-start.3
  1039.8 2.3 copy-start.19
  1040.2 2.7 copy-start.4
  1101.2 3.3 copy-start.5
  1101.2 3.3 copy-start.15
  1101.2 3.2 copy-start.31
  1103.4 162.9 %copy-start.35 = (f32[4,128,128]{1,2,0:T(8,128)S(1)}, f32[4,128,128]{1,2,0:T(8,128)}, u32[]{:S(2)}) copy-start(f32[4,128,128]{1,2,0:T(8,128)} %custom-call.40) | copy-start | bytes 786436
  1266.3 5.2 copy-start.6
  1269.1 4.4 copy-start.36
  1280.2 2.5 copy-start.1
  (22 other events, 34.7 us)
Sparse Core Ops, SparseCore 0:
  28.1 43.8 all-reduce.16
  78.2 229.7 all-reduce.14
  496.2 21.6 all-gather.1
  579.0 219.4 all-reduce.8
  812.8 220.9 all-reduce.10
  1045.4 220.8 all-reduce.12
where the time goes:
time: 1300 us; the launch traced here: 1290 us
  waiting for transfers between devices  798 us (61%)
  other arithmetic  337 us (26%)
  matrix products  80.9 us (6%)
  local copies, waits for them, and re-layouts  52.2 us (4%)
  between operations  20.5 us (2%)
    psum x4, waiting for transfers between devices, body(): corr = lax.psum(partial_corr, 'rows')  736 us
    another operation x6, other arithmetic, body(): delta = jax.scipy.linalg.cho_solve((factor, True), corr)  163 us
    another operation x30, other arithmetic, body(): jnp.linalg.cholesky(gram + ridge * identity_mat)  159 us
    another operation x53, local copies, waits for them, and re-layouts, body(): delta = jax.scipy.linalg.cho_solve((factor, True), corr)  42.4 us
    psum x1, waiting for transfers between devices, broadcast(): return lax.psum(jnp.where(mine, value, jnp.zeros_like(value)), axis)  40.5 us
    another operation x56, matrix products, body(): delta = jax.scipy.linalg.cho_solve((factor, True), corr)  34.4 us
  transfers between devices with their start and end apart: 6, of which 6 were waited for; matrix products, arithmetic and copies ran while one was open for 13% of the time, Pallas kernels for 0%

commit v1 on v0

v1 whole, which is shorter than its diff:
```python
import functools
import math

import jax
import jax.numpy as jnp
from jax import lax
from jax.experimental import pallas as pl
from jax.experimental.pallas import tpu as pltpu
from jax.sharding import PartitionSpec as P

MESH = pl.DeviceIdType.MESH
HIGHEST = lax.Precision.HIGHEST
ridge = 0.05

F = 512
LANES = 128
SLABS = F // LANES
BLOCKS = 9
DATA_ROWS = BLOCKS * SLABS * F

AXES = ((4, 32), (4, 8), (8, 1))


def coords():
    r = lax.axis_index("rows")
    return r, [lax.rem(r // stride, n) for n, stride in AXES]


def sibling():
    return {"blk": 1 - lax.axis_index("blk")}


COS_COEFS = None


def cos_turns(t):
    u = jnp.abs(t) - 0.25
    w = u * u
    acc = jnp.full_like(w, SIN_POLY[-1])
    for coef in SIN_POLY[-2::-1]:
        acc = acc * w + coef
    return acc * u


def fit_sin_poly():
    import numpy as np

    degree = 5
    nodes = (np.cos((np.arange(degree + 1) + 0.5) * np.pi / (degree + 1)) + 1.0) / 32.0
    root = np.sqrt(nodes)
    values = -np.sin(2 * np.pi * root) / root
    vander = np.vander(nodes, degree + 1, increasing=True)
    return [float(v) for v in np.linalg.solve(vander, values)]


SIN_POLY = fit_sin_poly()


def feature_kernel(scale, x_ref, projt_ref, phase_ref, y_ref, ft_ref, part_ref, send_sem, recv_sem):
    core = lax.axis_index("blk")
    rows = x_ref.shape[0]
    barrier = pltpu.get_barrier_semaphore()
    pl.semaphore_signal(barrier, inc=1, device_id=sibling(), device_id_type=MESH)
    pl.semaphore_wait(barrier, 1)

    chunk = 256
    copies = []
    for i in range(2):
        g = 2 * core + i

        def piece(j, _, i=i, g=g):
            cols = pl.ds(pl.multiple_of(j * chunk, chunk), chunk)
            pre = lax.dot_general(
                projt_ref[i], x_ref[cols, :], (((1,), (1,)), ((), ())), preferred_element_type=jnp.float32
            )
            turns = (pre + phase_ref[i]) * (0.5 / math.pi)
            turns = turns - jnp.round(turns)
            ft_ref[g, :, cols] = (cos_turns(turns) * scale).astype(jnp.bfloat16)
            return 0

        lax.fori_loop(0, rows // chunk, piece, 0)
        copy = pltpu.make_async_remote_copy(
            src_ref=ft_ref.at[g],
            dst_ref=ft_ref.at[g],
            send_sem=send_sem.at[i],
            recv_sem=recv_sem.at[i],
            device_id=sibling(),
            device_id_type=MESH,
        )
        copy.start()
        copies.append(copy)

    def put(q, half, value):
        for k in range(2):
            row = pl.multiple_of((q * SLABS + 2 * half + k) * F, F)
            part_ref[pl.ds(row, F), :] = value[:, k * LANES:(k + 1) * LANES]

    def gram(q, a, b):
        def one(half, _):
            cols = pl.ds(pl.multiple_of(half * 256, 256), 256)
            put(q, half, lax.dot_general(
                ft_ref[a], ft_ref[b, cols, :], (((1,), (1,)), ((), ())), preferred_element_type=jnp.float32
            ))
            return 0

        lax.fori_loop(0, 2, one, 0)

    def moment(b):
        def one(half, _):
            cols = pl.ds(pl.multiple_of(half * 256, 256), 256)
            put(5 + b, half, jnp.dot(ft_ref[b], y_ref[:, cols], preferred_element_type=jnp.float32))
            return 0

        lax.fori_loop(0, 2, one, 0)

    own = [2 * core, 2 * core + 1]
    other = [2 * (1 - core), 2 * (1 - core) + 1]
    gram(0, own[0], own[0])
    gram(1, own[1], own[1])
    gram(2, own[1], own[0])
    moment(own[0])
    moment(own[1])
    for i in range(2):
        pltpu.make_async_remote_copy(
            src_ref=ft_ref.at[own[i]],
            dst_ref=ft_ref.at[other[i]],
            send_sem=send_sem.at[i],
            recv_sem=recv_sem.at[i],
            device_id=sibling(),
            device_id_type=MESH,
        ).wait_recv()
    gram(3, 2, core)
    gram(4, 3, 1 - core)
    moment(other[0])
    moment(other[1])
    for copy in copies:
        copy.wait_send()


def features_and_parts(x, projt, phase, y):
    rows = x.shape[0]
    scale = 1.0 / math.sqrt(rows * 128)
    vmem = pl.BlockSpec(memory_space=pltpu.VMEM)
    return pl.pallas_call(
        functools.partial(feature_kernel, scale),
        out_shape=(
            jax.ShapeDtypeStruct((4, F, rows), jnp.bfloat16),
            jax.ShapeDtypeStruct((DATA_ROWS, LANES), jnp.float32),
        ),
        in_specs=[vmem] * 4,
        out_specs=(vmem, vmem),
        scratch_shapes=[pltpu.SemaphoreType.DMA((2,)), pltpu.SemaphoreType.DMA((2,))],
        compiler_params=pltpu.CompilerParams(
            collective_id=0, has_side_effects=True, vmem_limit_bytes=60 * 2**20
        ),
        name="features",
    )(x, projt, phase, y)


class Stream:
    def __init__(self, index, part, direction, base, length):
        self.index, self.dir, self.base = index, direction, base
        self.order = [(part + t) % 3 for t in range(3)]
        self.sizes = [AXES[a][0] for a in self.order]
        self.rows = []
        for n in self.sizes:
            length //= n
            self.rows.append(length)
        slot = base
        self.steps = []
        for t in range(3):
            for s in range(self.sizes[t] - 1):
                self.steps.append(("sum", t, s, slot))
                slot += self.rows[t]
        for t in (2, 1, 0):
            for s in range(self.sizes[t] - 1):
                self.steps.append(("gather", t, s, None))

    def slot_of(self, t, s):
        for kind, tt, ss, slot in self.steps:
            if kind == "sum" and (tt, ss) == (t, s):
                return slot


def add_rows(dst, dst_off, src, src_off, rows):
    step = rows
    for cand in (192, 128, 96):
        if rows > cand and rows % cand == 0:
            step = cand
            break
    if step == rows:
        dst[pl.ds(dst_off, rows), :] = dst[pl.ds(dst_off, rows), :] + src[pl.ds(src_off, rows), :]
        return

    def one(j, _):
        d = pl.ds(pl.multiple_of(dst_off + j * step, 8), step)
        s = pl.ds(pl.multiple_of(src_off + j * step, 8), step)
        dst[d, :] = dst[d, :] + src[s, :]
        return 0

    lax.fori_loop(0, rows // step, one, 0)


def plan(streams):
    events = []
    for st in streams:
        time = 0.0
        for k, (kind, t, s, slot) in enumerate(st.steps):
            time += 2.0 + st.rows[t] * LANES * 4 * 2 / 90e3
            events.append((time, st.index, k))
    return sorted(events)


def ring_kernel(streams, data_ref, out_ref, held, send_sem, recv_sem):
    r, here = coords()
    barrier = pltpu.get_barrier_semaphore()

    def neighbour(axis, direction):
        n, stride = AXES[axis]
        return {"rows": r + (lax.rem(here[axis] + n + direction, n) - here[axis]) * stride}

    for axis in range(3):
        for direction in (1, -1):
            pl.semaphore_signal(barrier, inc=1, device_id=neighbour(axis, direction), device_id_type=MESH)
    pl.semaphore_wait(barrier, 6)

    def aligned(v):
        return v if isinstance(v, int) else pl.multiple_of(v, 8)

    def chunk(st, t, back):
        n = st.sizes[t]
        return lax.rem(here[st.order[t]] - st.dir * back + 4 * n, n)

    def own_rows(st, t, k):
        if t == 0:
            return data_ref, aligned(st.base + k * st.rows[0])
        return held, aligned(st.slot_of(t - 1, st.sizes[t - 1] - 2) + k * st.rows[t])

    def out_rows(st, t, k):
        off = st.base
        for tt in range(t):
            off = off + here[st.order[tt]] * st.rows[tt]
        return aligned(off + k * st.rows[t])

    def make(st, k, receive=False):
        kind, t, s, slot = st.steps[k]
        rows = st.rows[t]
        axis = st.order[t]
        if kind == "sum":
            if s == 0:
                src, off = own_rows(st, t, chunk(st, t, 1))
            else:
                src, off = held, st.slot_of(t, s - 1)
            source = src.at[pl.ds(off, rows), :]
            dest = held.at[pl.ds(slot, rows), :]
        else:
            at = out_rows(st, t, chunk(st, t, s))
            if t == 2 and s == 0:
                source = held.at[pl.ds(st.slot_of(2, st.sizes[2] - 2), rows), :]
            else:
                source = out_ref.at[pl.ds(at, rows), :]
            if receive:
                at = out_rows(st, t, chunk(st, t, s + 1))
            dest = out_ref.at[pl.ds(at, rows), :]
        return pltpu.make_async_remote_copy(
            src_ref=source,
            dst_ref=dest,
            send_sem=send_sem.at[st.index, k],
            recv_sem=recv_sem.at[st.index, k],
            device_id=neighbour(axis, st.dir),
            device_id_type=MESH,
        )

    for st in streams:
        make(st, 0).start()
    for _, index, k in plan(streams):
        st = streams[index]
        kind, t, s, slot = st.steps[k]
        make(st, k, receive=True).wait_recv()
        if kind == "sum":
            src, off = own_rows(st, t, chunk(st, t, s + 2))
            add_rows(held, slot, src, off, st.rows[t])
        if k + 1 < len(st.steps):
            make(st, k + 1).start()
        if kind == "sum" and t == 2 and s == st.sizes[2] - 2:
            at = out_rows(st, 2, here[st.order[2]])
            out_ref[pl.ds(at, st.rows[2]), :] = held[pl.ds(slot, st.rows[2]), :]
    for st in streams:
        for k in range(len(st.steps)):
            make(st, k).wait_send()


def ring_sum(data):
    total = data.shape[0]
    length = total // 6
    streams = [Stream(2 * p + d, p, (1, -1)[d], (2 * p + d) * length, length) for p in range(3) for d in range(2)]
    nsteps = len(streams[0].steps)
    vmem = pl.BlockSpec(memory_space=pltpu.VMEM)
    return pl.pallas_call(
        functools.partial(ring_kernel, streams),
        out_shape=jax.ShapeDtypeStruct(data.shape, jnp.float32),
        in_specs=[vmem],
        out_specs=vmem,
        scratch_shapes=[
            pltpu.VMEM(data.shape, jnp.float32),
            pltpu.SemaphoreType.DMA((len(streams), nsteps)),
            pltpu.SemaphoreType.DMA((len(streams), nsteps)),
        ],
        compiler_params=pltpu.CompilerParams(
            collective_id=1, has_side_effects=True, vmem_limit_bytes=60 * 2**20
        ),
        name="ring_sum",
    )(data)


LOW, HIGH_EIG = 0.05, 130.0
NEWTON = 8


def base_inverses(mats):
    n = mats[0].shape[0]
    eye = (
        lax.broadcasted_iota(jnp.int32, (n, n), 0) == lax.broadcasted_iota(jnp.int32, (n, n), 1)
    ).astype(jnp.float32)
    c = 2.0 / (LOW + HIGH_EIG)
    rho = (HIGH_EIG - LOW) / (HIGH_EIG + LOW)

    def grow(rho):
        return rho * rho / (2.0 - rho * rho)

    s = 2.0 / (2.0 - rho * rho)
    xs = [s * (2.0 * c * eye - (c * c) * m) for m in mats]
    rho = grow(rho)

    def step(_, carry):
        xs, rho = carry
        s = 2.0 / (2.0 - rho * rho)
        nxt = []
        for m, x in zip(mats, xs):
            ax = jnp.dot(m, x, precision=HIGHEST, preferred_element_type=jnp.float32)
            xax = jnp.dot(x, ax, precision=HIGHEST, preferred_element_type=jnp.float32)
            nxt.append(s * (2.0 * x - xax))
        return tuple(nxt), rho * rho / (2.0 - rho * rho)

    xs, _ = lax.fori_loop(0, NEWTON, step, (tuple(xs), jnp.float32(rho)))
    return xs


def inverse_kernel(g_ref, out_ref):
    p = LANES
    for m in range(2):
        for k in range(SLABS):
            slab = g_ref[pl.ds((m * SLABS + k) * F, F), :]
            row = lax.broadcasted_iota(jnp.int32, (F, p), 0)
            col = lax.broadcasted_iota(jnp.int32, (F, p), 1) + k * p
            out_ref[m, :, k * p:(k + 1) * p] = jnp.where(row == col, slab + ridge, slab)
    for k in range(F // p):
        here = slice(k * p, (k + 1) * p)
        pivots = base_inverses([out_ref[m, here, here] for m in range(2)])
        for m in range(2):
            row = jnp.dot(pivots[m], out_ref[m, here, :], precision=HIGHEST, preferred_element_type=jnp.float32)
            col = out_ref[m, :, here]
            out_ref[m, :, here] = jnp.zeros_like(col)
            out_ref[m, here, :] = row
            out_ref[m, here, here] = pivots[m]
            full = out_ref[m, here, :]
            for i in range(F // p):
                if i != k:
                    rows = slice(i * p, (i + 1) * p)
                    out_ref[m, rows, :] = out_ref[m, rows, :] - jnp.dot(
                        col[rows], full, precision=HIGHEST, preferred_element_type=jnp.float32
                    )


def inverses(summed):
    return pl.pallas_call(
        inverse_kernel,
        out_shape=jax.ShapeDtypeStruct((2, F, F), jnp.float32),
        grid=(1,),
        in_specs=[pl.BlockSpec((2 * SLABS * F, LANES), lambda i: (0, 0))],
        out_specs=pl.BlockSpec((2, F, F), lambda i: (0, 0, 0)),
        compiler_params=pltpu.CompilerParams(vmem_limit_bytes=48 * 2**20),
        name="inverses",
    )(summed)


def split(value):
    high = value.astype(jnp.bfloat16)
    return high, (value - high.astype(jnp.float32)).astype(jnp.bfloat16)


def dot(a, b):
    return jnp.dot(a, b, preferred_element_type=jnp.float32)


def sweep_kernel(inv_ref, inv2_ref, g_ref, g2_ref, c_ref, ft_ref, y_ref, coef_ref, res_ref,
                 ih, il, gh, gl):
    core = lax.axis_index("blk")
    for own, (iref, gref) in enumerate(((inv_ref, g_ref), (inv2_ref, g2_ref))):
        owner = core if own == 0 else 1 - core
        for k in range(2):
            high, low = split(iref[k])
            ih[2 * owner + k] = high
            il[2 * owner + k] = low
        for k in range(3):
            for j in range(SLABS):
                high, low = split(gref[pl.ds((k * SLABS + j) * F, F), :])
                cols = slice(j * LANES, (j + 1) * LANES)
                gh[3 * owner + k, :, cols] = high
                gl[3 * owner + k, :, cols] = low
    where = {(1, 0): 0, (2, 0): 1, (3, 1): 2, (3, 2): 3, (2, 1): 4, (3, 0): 5}

    def one(half, _):
        cols = pl.ds(pl.multiple_of(half * 256, 256), 256)
        rounded = []
        for b in range(4):
            corr = jnp.concatenate(
                [
                    c_ref[pl.ds(pl.multiple_of((b * SLABS + 2 * half + k) * F, F), F), :]
                    for k in range(2)
                ],
                axis=1,
            )
            for j in range(b):
                corr = corr - (dot(gh[where[b, j]], rounded[j]) + dot(gl[where[b, j]], rounded[j]))
            ch, cl = split(corr)
            delta = dot(ih[b], ch) + (dot(ih[b], cl) + dot(il[b], ch))
            coef_ref[b, :, cols] = delta
            rounded.append(delta.astype(jnp.bfloat16))
        fit = lax.dot_general(
            ft_ref[0], rounded[0], (((0,), (0,)), ((), ())), preferred_element_type=jnp.float32
        )
        for b in range(1, 4):
            fit = fit + lax.dot_general(
                ft_ref[b], rounded[b], (((0,), (0,)), ((), ())), preferred_element_type=jnp.float32
            )
        res_ref[:, cols] = y_ref[:, cols].astype(jnp.float32) - fit
        return 0

    lax.fori_loop(0, 2, one, 0)


def sweep(inv, inv2, g, g2, c, ft, y):
    vmem = pl.BlockSpec(memory_space=pltpu.VMEM)
    return pl.pallas_call(
        sweep_kernel,
        out_shape=(
            jax.ShapeDtypeStruct((4, F, y.shape[1]), jnp.float32),
            jax.ShapeDtypeStruct(y.shape, jnp.float32),
        ),
        in_specs=[vmem] * 7,
        out_specs=(vmem, vmem),
        scratch_shapes=[
            pltpu.VMEM((4, F, F), jnp.bfloat16),
            pltpu.VMEM((4, F, F), jnp.bfloat16),
            pltpu.VMEM((6, F, F), jnp.bfloat16),
            pltpu.VMEM((6, F, F), jnp.bfloat16),
        ],
        compiler_params=pltpu.CompilerParams(vmem_limit_bytes=62 * 2**20),
        name="sweep",
    )(inv, inv2, g, g2, c, ft, y)


def body(inputs, proj, phase, targets):
    projt = jnp.swapaxes(proj, 1, 2)
    shift = phase.astype(jnp.float32)[:, :, None]
    ft, parts = features_and_parts(inputs, projt, shift, targets)
    summed = ring_sum(parts)
    inv = inverses(summed)
    cross = summed[2 * SLABS * F:5 * SLABS * F]
    moments = summed[5 * SLABS * F:]
    swap = [(0, 1), (1, 0)]
    cross2 = lax.ppermute(cross, "blk", swap)
    inv2 = lax.ppermute(inv, "blk", swap)
    return sweep(inv, inv2, cross, cross2, moments, ft, targets)


def solution(mesh):
    return jax.shard_map(
        body,
        mesh=mesh,
        in_specs=(P("rows", None), P("blk", None, None), P("blk", None), P("rows", "blk")),
        out_specs=(P(None, None, "blk"), P("rows", "blk")),
        check_vma=False,
    )
```

time: 1300 us -> 355 us (0.27)
  waiting for transfers between devices: 798 us -> 0.01 us
  other arithmetic: 337 us -> 0.69 us
  Pallas kernels: 0 us -> 321 us
  matrix products: 80.9 us -> 0 us
  local copies, waits for them, and re-layouts: 52.2 us -> 16.4 us
  between operations: 20.5 us -> 0.69 us
    psum x5 -> x0, waiting for transfers between devices: 776 us -> none  [the longest x4 736 us: body(): corr = lax.psum(partial_corr, 'rows')]
    another operation x44 -> x0, other arithmetic: 332 us -> none  [the longest x6 163 us: body(): delta = jax.scipy.linalg.cho_solve((factor, True), corr)]
    pallas_call x0 -> x4, Pallas kernels: none -> 321 us  [the longest x1 247 us: ring_sum(): pl.pallas_call(functools.partial(ring_kernel, streams), out_shape=jax.Sha...]
    another operation x68 -> x0, matrix products: 45.3 us -> none  [the longest x56 34.4 us: body(): delta = jax.scipy.linalg.cho_solve((factor, True), corr)]
    another operation x61 -> x0, local copies, waits for them, and re-layouts: 42.7 us -> none  [the longest x53 42.4 us: body(): delta = jax.scipy.linalg.cho_solve((factor, True), corr)]
    dot_general x12 -> x0, matrix products: 35.5 us -> none  [the longest x2 19.5 us: build(): jnp.dot(inputs, weights, preferred_element_type=jnp.float32)]
    all_gather x1 -> x0, waiting for transfers between devices: 21.8 us -> none  [body(): factors = lax.all_gather(own_factors, 'blk', axis=0, tiled=True)]
    ppermute x0 -> x2, starting transfers between devices: none -> 13.5 us  [the longest x1 12.7 us: body(): cross2 = lax.ppermute(cross, 'blk', swap)]
  transfers between devices with their start and end apart: 6 -> 2, of which waited for: 6 -> 0; matrix products, arithmetic and copies ran while one was open for 13% -> 1% of each run, Pallas kernels for 0% -> 8%
where the time goes in v1:
time: 355 us; the launch traced here: 352 us
  Pallas kernels  321 us (90%)
  local copies, waits for them, and re-layouts  16.4 us (5%)
  starting transfers between devices  13.5 us (4%)
    pallas_call x1, Pallas kernels, ring_sum(): pl.pallas_call(functools.partial(ring_kernel, streams), out_shape=jax.Sha...  247 us
    pallas_call x1, Pallas kernels, inverses(): pl.pallas_call(inverse_kernel, out_shape=jax.ShapeDtypeStruct((2, F, F),...  28.2 us
    pallas_call x1, Pallas kernels, features_and_parts(): pl.pallas_call(functools.partial(feature_kernel, scale), out_shape=(jax.S...  22.9 us
    pallas_call x1, Pallas kernels, sweep(): pl.pallas_call(sweep_kernel, out_shape=(jax.ShapeDtypeStruct((4, F, y.sha...  22.7 us
    ppermute x1, starting transfers between devices, body(): cross2 = lax.ppermute(cross, 'blk', swap)  12.7 us
    unnamed x10, local copies, waits for them, and re-layouts  8.8 us
  transfers between devices with their start and end apart: 2, of which 0 were waited for; matrix products, arithmetic and copies ran while one was open for 1% of the time, Pallas kernels for 8%

profile of v1, /device:TPU:1, one launch (start us, length us, event | category | flops | bytes accessed | tf_op | source)
XLA Modules:
  0.0 352.1 jit_solution(18047998590496506101)
XLA Ops:
  0.6 0.7 bitcast_convert_fusion
  1.3 1.0 copy.10.phase_ref
  2.3 2.2 copy.9.x_ref
  4.6 2.2 copy.8
  6.8 22.9 %features.1 = (bf16[4,512,1024]{2,1,0:T(8,128)(2,1)}, f32[18432,128]{1,0:T(8,128)}) custom-call(bf16[1024,440]{1,0:T(8,128)(2,1)} %copy.9.x_ref, bf16[2,512,440]{2,1,0:T(8,128)(2,1)} %bitcast.4, f32[2,512,1]{2,1,0:T(8,128)} %copy.10.phase_ref, bf16[1024,512]{1,0:T(8,128)(2,1)} %y_ref.3), custom_call_target="tpu_custom_call" | custom-call | tf_op jit(solution)/shard_map/features/pallas_call | solution.py:144
  29.8 246.9 %ring_sum.1.g_ref = f32[18432,128]{1,0:T(8,128)} custom-call(f32[18432,128]{1,0:T(8,128)} %get-tuple-element.4.data_ref), custom_call_target="tpu_custom_call" | custom-call | tf_op jit(solution)/shard_map/ring_sum/pallas_call | solution.py:299
  276.7 2.1 slice.6.g_ref
  278.8 0.0 copy-start.1
  278.8 12.7 %collective-permute-start.1 = (f32[6144,128]{1,0:T(8,128)S(1)}, f32[6144,128]{1,0:T(8,128)S(1)}, u32[]{:S(2)}, u32[]{:S(2)}) collective-permute-start(f32[6144,128]{1,0:T(8,128)S(1)} %slice.6.g_ref), channel_id=1, source_target_pairs={{0,1},{1,0},{2,3},{3,2},{4,5},{5,4},{6,7},{7,6},{8,9},{9,8},{10,11... | collective-permute-start | bytes 9437192 | tf_op jit(solution)/shard_map/ppermute | solution.py:473
  291.4 28.2 %inverses.1.inv_ref = f32[2,512,512]{2,1,0:T(8,128)S(1)} custom-call(f32[18432,128]{1,0:T(8,128)} %ring_sum.1.g_ref), custom_call_target="tpu_custom_call" | custom-call | tf_op jit(solution)/shard_map/inverses/pallas_call | solution.py:376
  319.7 0.0 copy-done.1
  319.7 0.0 copy-start
  319.7 1.3 copy-done
  321.1 0.9 collective-permute-start
  321.9 4.5 %slice.7.c_ref = f32[8192,128]{1,0:T(8,128)} slice(f32[18432,128]{1,0:T(8,128)} %ring_sum.1.g_ref), slice={[10240:18432], [0:128]} | slice | bytes 8388608 | tf_op jit(solution)/shard_map/slice | solution.py:471
  326.4 0.0 collective-permute-done.inv2_ref
  326.4 0.0 copy-start.3
  326.4 0.0 collective-permute-done.1.g2_ref
  326.4 1.3 copy-done.3
  327.8 0.0 copy-start.2
  327.8 1.6 copy-done.2
  329.4 22.7 %sweep.1 = (f32[4,512,512]{2,1,0:T(8,128)}, f32[1024,512]{1,0:T(8,128)}) custom-call(f32[2,512,512]{2,1,0:T(8,128)} %copy-done, f32[2,512,512]{2,1,0:T(8,128)} %copy-done.3, f32[6144,128]{1,0:T(8,128)} %copy-done.1, f32[6144,128]{1,0:T(8,128)} %copy-done.2, f32[8192,128]{1,0:T(8,128)} %slice.7.c_ref, bf16[4,512,1024]{2,1,0:T(8,128)(2,1)} %get-tuple-element.5.ft_ref, ...), custom_call_target="tpu_custom_call" | custom-call | tf_op jit(solution)/shard_map/sweep/pallas_call | solution.py:445
Async XLA Ops:
  278.8 40.9 %copy-start.1 = (f32[6144,128]{1,0:T(8,128)}, f32[6144,128]{1,0:T(8,128)S(1)}, u32[]{:S(2)}) copy-start(f32[6144,128]{1,0:T(8,128)S(1)} %slice.6.g_ref) | copy-start | bytes 9437188
  278.8 47.7 %collective-permute-start.1 = (f32[6144,128]{1,0:T(8,128)S(1)}, f32[6144,128]{1,0:T(8,128)S(1)}, u32[]{:S(2)}, u32[]{:S(2)}) collective-permute-start(f32[6144,128]{1,0:T(8,128)S(1)} %slice.6.g_ref), channel_id=1, source_target_pairs={{0,1},{1,0},{2,3},{3,2},{4,5},{5,4},{6,7},{7,6},{8,9},{9,8},{10,11... | collective-permute-start | bytes 9437192 | tf_op jit(solution)/shard_map/ppermute | solution.py:473
  319.7 1.4 copy-start
  321.1 5.4 %collective-permute-start = (f32[2,512,512]{2,1,0:T(8,128)S(1)}, f32[2,512,512]{2,1,0:T(8,128)S(1)}, u32[]{:S(2)}, u32[]{:S(2)}) collective-permute-start(f32[2,512,512]{2,1,0:T(8,128)S(1)} %inverses.1.inv_ref), channel_id=1, source_target_pairs={{0,1},{1,0},{2,3},{3,2},{4,5},{5,4},{6,7},{7,6},{8,9},{9,8},{10,11... | collective-permute-start | bytes 6291464 | tf_op jit(solution)/shard_map/ppermute | solution.py:474
  326.4 1.3 copy-start.3
  327.8 1.6 copy-start.2

commit v2 on v0

v2 whole, which is shorter than its diff:
```python
import functools
import math

import jax
import jax.numpy as jnp
from jax import lax
from jax.experimental import pallas as pl
from jax.experimental.pallas import tpu as pltpu
from jax.sharding import PartitionSpec as P

MESH = pl.DeviceIdType.MESH
LOGICAL = pl.DeviceIdType.LOGICAL
HIGHEST = lax.Precision.HIGHEST
ridge = 0.05

F = 512
LANES = 128
SLABS = F // LANES
TILES = SLABS * (SLABS + 1) // 2
CROSS = 2 * TILES * LANES
MOMENT = CROSS + 3 * SLABS * F
DATA_ROWS = MOMENT + 4 * SLABS * F


def tile_row(m, i, j):
    return (m * TILES + i * (i + 1) // 2 + j) * LANES


def sibling():
    return {"blk": 1 - lax.axis_index("blk")}


def cos_turns(t):
    u = jnp.abs(t) - 0.25
    w = u * u
    acc = jnp.full_like(w, SIN_POLY[-1])
    for coef in SIN_POLY[-2::-1]:
        acc = acc * w + coef
    return acc * u


def fit_sin_poly():
    import numpy as np

    degree = 5
    nodes = (np.cos((np.arange(degree + 1) + 0.5) * np.pi / (degree + 1)) + 1.0) / 32.0
    root = np.sqrt(nodes)
    values = -np.sin(2 * np.pi * root) / root
    vander = np.vander(nodes, degree + 1, increasing=True)
    return [float(v) for v in np.linalg.solve(vander, values)]


SIN_POLY = fit_sin_poly()


def feature_kernel(scale, xt_ref, proj_ref, phase_ref, y_ref, ft_ref, part_ref, send_sem, recv_sem):
    core = lax.axis_index("blk")
    rows = xt_ref.shape[1]
    barrier = pltpu.get_barrier_semaphore()
    pl.semaphore_signal(barrier, inc=1, device_id=sibling(), device_id_type=MESH)
    pl.semaphore_wait(barrier, 1)

    chunk = 256
    copies = []
    for i in range(2):
        g = 2 * core + i
        shift = jnp.broadcast_to(phase_ref[i:i + 1, :].astype(jnp.float32), (8, F)).T[:, :1]

        def piece(j, _, i=i, g=g, shift=shift):
            cols = pl.ds(pl.multiple_of(j * chunk, chunk), chunk)
            pre = lax.dot_general(
                proj_ref[i], xt_ref[:, cols], (((0,), (0,)), ((), ())), preferred_element_type=jnp.float32
            )
            turns = (pre + shift) * (0.5 / math.pi)
            turns = turns - jnp.round(turns)
            ft_ref[g, :, cols] = (cos_turns(turns) * scale).astype(jnp.bfloat16)
            return 0

        lax.fori_loop(0, rows // chunk, piece, 0)
        copy = pltpu.make_async_remote_copy(
            src_ref=ft_ref.at[g],
            dst_ref=ft_ref.at[g],
            send_sem=send_sem.at[i],
            recv_sem=recv_sem.at[i],
            device_id=sibling(),
            device_id_type=MESH,
        )
        copy.start()
        copies.append(copy)

    def put(base, half, value):
        for k in range(2):
            row = pl.multiple_of(base + (2 * half + k) * F, LANES)
            part_ref[pl.ds(row, F), :] = value[:, k * LANES:(k + 1) * LANES]

    def diagonal(m, a):
        for half in range(2):
            top = 256 * half
            value = lax.dot_general(
                ft_ref[a, top:, :], ft_ref[a, top:top + 256, :], (((1,), (1,)), ((), ())),
                preferred_element_type=jnp.float32,
            )
            for k in range(2):
                j = 2 * half + k
                for i in range(j, SLABS):
                    rows = slice(i * LANES - top, (i + 1) * LANES - top)
                    part_ref[pl.ds(tile_row(m, i, j), LANES), :] = value[rows, k * LANES:(k + 1) * LANES]

    def gram(q, a, b):
        def one(half, _):
            cols = pl.ds(pl.multiple_of(half * 256, 256), 256)
            put(CROSS + q * SLABS * F, half, lax.dot_general(
                ft_ref[a], ft_ref[b, cols, :], (((1,), (1,)), ((), ())), preferred_element_type=jnp.float32
            ))
            return 0

        lax.fori_loop(0, 2, one, 0)

    def moment(b):
        def one(half, _):
            cols = pl.ds(pl.multiple_of(half * 256, 256), 256)
            put(MOMENT + b * SLABS * F, half, jnp.dot(ft_ref[b], y_ref[:, cols], preferred_element_type=jnp.float32))
            return 0

        lax.fori_loop(0, 2, one, 0)

    own = [2 * core, 2 * core + 1]
    other = [2 * (1 - core), 2 * (1 - core) + 1]
    diagonal(0, own[0])
    diagonal(1, own[1])
    gram(0, own[1], own[0])
    moment(own[0])
    moment(own[1])
    for i in range(2):
        pltpu.make_async_remote_copy(
            src_ref=ft_ref.at[own[i]],
            dst_ref=ft_ref.at[other[i]],
            send_sem=send_sem.at[i],
            recv_sem=recv_sem.at[i],
            device_id=sibling(),
            device_id_type=MESH,
        ).wait_recv()
    gram(1, 2, core)
    gram(2, 3, 1 - core)
    moment(other[0])
    moment(other[1])
    for copy in copies:
        copy.wait_send()


def features_and_parts(xt, proj, phase, y):
    rows = xt.shape[1]
    scale = 1.0 / math.sqrt(rows * 128)
    vmem = pl.BlockSpec(memory_space=pltpu.VMEM)
    return pl.pallas_call(
        functools.partial(feature_kernel, scale),
        out_shape=(
            jax.ShapeDtypeStruct((4, F, rows), jnp.bfloat16),
            jax.ShapeDtypeStruct((DATA_ROWS, LANES), jnp.float32),
        ),
        in_specs=[vmem] * 4,
        out_specs=(vmem, vmem),
        scratch_shapes=[pltpu.SemaphoreType.DMA((2,)), pltpu.SemaphoreType.DMA((2,))],
        compiler_params=pltpu.CompilerParams(
            collective_id=0, has_side_effects=True, vmem_limit_bytes=60 * 2**20
        ),
        name="features",
    )(xt, proj, phase, y)


AXES = ((4, 32), (8, 4), (4, 1))
Y, Z, X = 0, 1, 2
PARTS = (((Y, X, Z), None), ((Z, X), Y), ((X, Y, Z), None))


def coords():
    r = lax.axis_index("rows")
    return r, [lax.rem(r // stride, n) for n, stride in AXES]


class Stream:
    def __init__(self, index, part, direction, base, length, held, modes):
        self.index, self.dir, self.base = index, direction, base
        self.order, last = PARTS[part]
        depth = len(self.order)
        self.rows = []
        for a in self.order:
            length //= AXES[a][0]
            self.rows.append(length)
        assert length % 8 == 0
        scatter = [("rs", a, i, self.rows[i], modes[part][i]) for i, a in enumerate(self.order)]
        middle = [] if last is None else [("ar", last, depth - 1, self.rows[-1], "direct")]
        gather = [("ag", a, i, rows, mode) for _, a, i, rows, mode in scatter[::-1]]
        self.stages = scatter + middle + gather
        self.final = len(scatter + middle) - 1
        self.first, self.slots, count = [], [], 0
        for kind, axis, pos, rows, mode in self.stages:
            n = AXES[axis][0]
            self.first.append(count)
            count += n - 1
            if kind != "ag":
                self.slots.append([held + s * rows for s in range(n - 1)])
                held += (n - 1) * rows
        self.count, self.held_end = count, held
        self.sums = [
            slots[-1 if self.stages[t][4] == "ring" else 0] for t, slots in enumerate(self.slots)
        ]
        self.events = []
        for g, (kind, axis, pos, rows, mode) in enumerate(self.stages):
            n = AXES[axis][0]
            after = self.initial(g + 1)
            if mode == "ring":
                for s in range(n - 1):
                    self.events.append(([(g, s)], (g, s), [(g, s + 1)] if s < n - 2 else after))
            else:
                self.events.append(([(g, s) for s in range(n - 1)], (g, None), after))

    def initial(self, g):
        if g >= len(self.stages):
            return []
        n = AXES[self.stages[g][1]][0]
        return [(g, 0)] if self.stages[g][4] == "ring" else [(g, s) for s in range(n - 1)]


class Plan:
    def __init__(self, rounds, latency=2.4, rate=47e3, extra=()):
        self.streams, held, base = [], 0, 0
        for number, (units, modes, delay) in enumerate(rounds):
            for part in range(3):
                for d in range(2):
                    length = units[part]
                    if not length:
                        continue
                    st = Stream(len(self.streams), part, (1, -1)[d], base, length, held, modes)
                    st.round, st.delay = number, delay
                    held = st.held_end
                    base += length
                    self.streams.append(st)
        self.held, self.rows = held, base
        self.copies = max(st.count for st in self.streams)
        self.simulate(latency, rate, extra)

    def simulate(self, latency, rate, extra=()):
        free, order, ready, core = {}, [], [], 0.0
        arrival = {}

        def send(st, copy, now):
            g, s = copy
            kind, axis, pos, rows, mode = st.stages[g]
            n = AXES[axis][0]
            hops, direction = 1, st.dir
            if mode == "direct":
                hops = min(s + 1, n - s - 1)
                direction = 1 if s + 1 <= n // 2 else -1
            link = (axis, direction)
            start = max(now, free.get(link, 0.0))
            free[link] = start + hops * rows * LANES * 4 / rate
            arrival[st.index, copy] = free[link] + latency + 0.8 * (hops - 1)

        nxt = {}
        for st in self.streams:
            nxt[st.index] = -1
        pieces, done0 = list(extra), len([s for s in self.streams if s.round == 0])
        self.round_end = {}
        while True:
            best = None
            for st in self.streams:
                e = nxt[st.index]
                if e >= len(st.events):
                    continue
                when = st.delay if e < 0 else max(arrival[st.index, c] for c in st.events[e][0])
                key = (max(when, core), st.round, when, st.index)
                if best is None or key < best[0]:
                    best = (key, st)
            if best is None:
                break
            if pieces and done0 == 0 and best[0][0] > core + 0.3:
                core += pieces.pop(0)
                order.append(("piece", None))
                continue
            when, st = best[0][0], best[1]
            e = nxt[st.index]
            core = when + 0.1
            order.append((st.index, e))
            for copy in (st.initial(0) if e < 0 else st.events[e][2]):
                send(st, copy, core)
            nxt[st.index] += 1
            if nxt[st.index] >= len(st.events):
                self.round_end[st.round] = core
                if st.round == 0:
                    done0 -= 1
                order.append(("end", st.index))
        for _ in pieces:
            order.append(("piece", None))
        self.order, self.time = order, core + sum(pieces)


def add_into(dst, dst_off, terms, rows):
    step = rows
    for cand in (192, 144, 128, 96, 72, 64):
        if rows > cand and rows % cand == 0:
            step = cand
            break

    def value(term, j):
        if isinstance(term[0], tuple):
            total = value(term[0], j)
            for other in term[1:]:
                total = total + value(other, j)
            return total
        ref, off = term
        return ref[pl.ds(aligned(off + j * step), step), :]

    def one(j, _):
        dst[pl.ds(aligned(dst_off + j * step), step), :] = value(terms, j)
        return 0

    if step == rows:
        one(0, 0)
    else:
        lax.fori_loop(0, rows // step, one, 0)


def aligned(v):
    return v if isinstance(v, int) else pl.multiple_of(v, 8)


class Ring:
    def __init__(self, plan, data_ref, out_ref, held, send_sem, recv_sem):
        self.plan, self.data, self.out, self.held = plan, data_ref, out_ref, held
        self.send_sem, self.recv_sem = send_sem, recv_sem
        self.r, self.here = coords()
        core = lax.axis_index("blk")
        self.chunks, self.ids, self.bases = {}, {}, {}
        for axis, (n, stride) in enumerate(AXES):
            for offset in range(n):
                k = lax.rem(self.here[axis] + offset, n) if offset else self.here[axis]
                self.chunks[axis, offset] = k
                self.ids[axis, offset] = 2 * (self.r + (k - self.here[axis]) * stride) + core

    def neighbour(self, axis, offset):
        return self.ids[axis, offset % AXES[axis][0]]

    def chunk(self, axis, offset):
        return self.chunks[axis, offset % AXES[axis][0]]

    def own(self, st, g, k):
        if g == 0:
            return self.data, aligned(st.base + k * st.rows[0])
        return self.held, aligned(st.sums[g - 1] + k * st.rows[g])

    def place(self, st, pos, k):
        if (st.index, pos) not in self.bases:
            off = st.base
            for i in range(pos):
                off = off + self.here[st.order[i]] * st.rows[i]
            self.bases[st.index, pos] = off
        return aligned(self.bases[st.index, pos] + k * st.rows[pos])

    def copy(self, st, copy, receive=False):
        g, s = copy
        kind, axis, pos, rows, mode = st.stages[g]
        ring = mode == "ring"
        target = st.dir if ring else s + 1
        if kind == "rs":
            if ring and s > 0:
                src = self.held, st.slots[g][s - 1]
            else:
                src = self.own(st, g, self.chunk(axis, -st.dir if ring else s + 1))
            dst = self.held, st.slots[g][s]
        elif kind == "ar":
            src = self.held, st.sums[g - 1]
            dst = self.held, st.slots[g][s]
        else:
            ahead = -st.dir * s if ring else 0
            back = -st.dir * (s + 1) if ring else -(s + 1)
            src = self.out, self.place(st, pos, self.chunk(axis, ahead))
            dst = self.out, self.place(st, pos, self.chunk(axis, back if receive else ahead))
        return pltpu.make_async_remote_copy(
            src_ref=src[0].at[pl.ds(src[1], rows), :],
            dst_ref=dst[0].at[pl.ds(dst[1], rows), :],
            send_sem=self.send_sem.at[st.index, st.first[g] + s],
            recv_sem=self.recv_sem.at[st.index, st.first[g] + s],
            device_id=self.neighbour(axis, target),
            device_id_type=LOGICAL,
        )

    def event(self, index, e):
        st = self.plan.streams[index]
        if e < 0:
            for c in st.initial(0):
                self.copy(st, c).start()
            return
        waits, (g, s), sends = st.events[e]
        for c in waits:
            self.copy(st, c, receive=True).wait_recv()
        kind, axis, pos, rows, mode = st.stages[g]
        if kind != "ag":
            final = g == st.final and s in (None, AXES[axis][0] - 2)
            if kind == "ar":
                a, b, c = [(self.held, slot) for slot in st.slots[g]]
                terms = (((self.held, st.sums[g - 1]), b), (a, c))
            elif s is None:
                own = self.own(st, g, self.chunk(axis, 0))
                terms = (own,) + tuple((self.held, slot) for slot in st.slots[g])
            else:
                own = self.own(st, g, self.chunk(axis, -st.dir * (s + 2)))
                terms = ((self.held, st.slots[g][s]), own)
            if final:
                dst = self.out, self.place(st, pos, self.chunk(axis if kind == "rs" else st.order[pos], 0))
            else:
                dst = self.held, st.slots[g][s or 0]
            add_into(*dst, terms, rows)
        for c in sends:
            self.copy(st, c).start()

    def finish(self):
        for st in self.plan.streams:
            for g in range(len(st.stages)):
                for s in range(AXES[st.stages[g][1]][0] - 1):
                    self.copy(st, (g, s)).wait_send()

    def devices(self):
        for axis, (n, _) in enumerate(AXES):
            for offset in range(1, n):
                yield self.neighbour(axis, offset)


LOW, HIGH_EIG = 0.05, 130.0
NEWTON = 8


def newton_scales():
    rho = (HIGH_EIG - LOW) / (HIGH_EIG + LOW)
    scales = []
    for _ in range(NEWTON + 1):
        scales.append(2.0 / (2.0 - rho * rho))
        rho = rho * rho / (2.0 - rho * rho)
    return scales


def mm(a, b):
    return jnp.dot(a, b, precision=HIGHEST, preferred_element_type=jnp.float32)


def split(value):
    high = value.astype(jnp.bfloat16)
    return high, (value - high.astype(jnp.float32)).astype(jnp.bfloat16)


class Inverses:
    def __init__(self, src, work, pivot):
        self.src, self.work, self.pivot = src, work, pivot
        self.scales = newton_scales()

    @staticmethod
    def durations():
        return [1.0] + SLABS * ([0.3] + (NEWTON // 2) * [1.4] + [0.8, 0.8])

    def pieces(self):
        yield self.load
        for k in range(SLABS):
            yield functools.partial(self.start, k)
            for i in range(NEWTON // 2):
                yield functools.partial(self.newton, k, i)
            for m in range(2):
                yield functools.partial(self.update, k, m)

    def eye(self):
        shape = (LANES, LANES)
        return lax.broadcasted_iota(jnp.int32, shape, 0) == lax.broadcasted_iota(jnp.int32, shape, 1)

    def load(self):
        eye = jnp.where(self.eye(), jnp.float32(ridge), jnp.float32(0.0))
        for m in range(2):
            for i in range(SLABS):
                for j in range(i + 1):
                    tile = self.src[pl.ds(tile_row(m, i, j), LANES), :]
                    a, b = slice(i * LANES, (i + 1) * LANES), slice(j * LANES, (j + 1) * LANES)
                    if i == j:
                        self.work[m, a, b] = tile + eye
                    else:
                        self.work[m, a, b] = tile
                        self.work[m, b, a] = tile.T

    def start(self, k):
        here = slice(k * LANES, (k + 1) * LANES)
        c, s = 2.0 / (LOW + HIGH_EIG), self.scales[0]
        for m in range(2):
            self.pivot[m] = jnp.where(self.eye(), jnp.float32(2.0 * c * s), jnp.float32(0.0)) - (c * c * s) * self.work[m, here, here]

    def newton(self, k, i):
        here = slice(k * LANES, (k + 1) * LANES)
        first, second = self.scales[1 + 2 * i], self.scales[2 + 2 * i]

        def step(t, _):
            s = jnp.where(t == 0, jnp.float32(first), jnp.float32(second))
            xs = [self.pivot[m] for m in range(2)]
            ax = [mm(self.work[m, here, here], xs[m]) for m in range(2)]
            xax = [mm(xs[m], ax[m]) for m in range(2)]
            for m in range(2):
                self.pivot[m] = s * (2.0 * xs[m] - xax[m])
            return 0

        lax.fori_loop(0, 2, step, 0)

    def update(self, k, m):
        here = slice(k * LANES, (k + 1) * LANES)
        work, inv = self.work, self.pivot[m]
        row = mm(inv, work[m, here, :])
        col = work[m, :, here]
        work[m, :, here] = jnp.zeros_like(col)
        work[m, here, :] = row
        work[m, here, here] = inv
        full = work[m, here, :]
        for i in range(SLABS):
            if i != k:
                rows = slice(i * LANES, (i + 1) * LANES)
                work[m, rows, :] = work[m, rows, :] - mm(col[rows], full)


def sum_kernel(plan, data_ref, out_ref, cross_ref, high_ref, low_ref, held, work, pivot,
               send_sem, recv_sem, pair_send, pair_recv):
    ring = Ring(plan, data_ref, out_ref, held, send_sem, recv_sem)
    core = lax.axis_index("blk")
    other = 2 * ring.r + 1 - core
    barrier = pltpu.get_barrier_semaphore()
    met = 1
    pl.semaphore_signal(barrier, inc=1, device_id=other, device_id_type=LOGICAL)
    for device in ring.devices():
        pl.semaphore_signal(barrier, inc=1, device_id=device, device_id_type=LOGICAL)
        met += 1
    pl.semaphore_wait(barrier, met)

    def pair(slot, src, dst):
        return pltpu.make_async_remote_copy(
            src_ref=src, dst_ref=dst, send_sem=pair_send.at[slot], recv_sem=pair_recv.at[slot],
            device_id=other, device_id_type=LOGICAL,
        )

    def cross(slot):
        start, rows = ((0, SLABS * F), (SLABS * F, 2 * SLABS * F))[slot]
        return pair(slot, out_ref.at[pl.ds(CROSS + start, rows), :], cross_ref.at[pl.ds(start, rows), :])

    inverses = Inverses(out_ref, work, pivot)
    pieces = inverses.pieces()
    left = [sum(st.round == n for st in plan.streams) for n in range(3)]
    for what, arg in plan.order:
        if what == "piece":
            next(pieces)()
        elif what == "end":
            n = plan.streams[arg].round
            left[n] -= 1
            if n < 2 and left[n] == 0:
                cross(n).start()
        else:
            ring.event(what, arg)
    for m in range(2):
        high, low = split(work[m])
        high_ref[2 * core + m] = high
        low_ref[2 * core + m] = low
    for k, ref in enumerate((high_ref, low_ref)):
        pair(2 + k, ref.at[pl.ds(2 * core, 2)], ref.at[pl.ds(2 * core, 2)]).start()
    ring.finish()
    for slot in range(2):
        cross(slot).wait()
    for k, ref in enumerate((high_ref, low_ref)):
        pair(2 + k, ref.at[pl.ds(2 * core, 2)], ref.at[pl.ds(2 * (1 - core), 2)]).wait()


def mode(first, second, middle):
    return ((first, second, "direct"), (middle, second), (first, second, "direct"))


ROUNDS = (
    ((1024, 256, 1024), mode("ring", "direct", "ring"), 0.0),
    ((1024, 1024, 1024), mode("ring", "ring", "ring"), 1.0),
    ((1024, 1024, 1024), mode("ring", "ring", "ring"), 2.0),
)


def sum_and_invert(data):
    plan = Plan(ROUNDS, extra=Inverses.durations())
    assert plan.rows == data.shape[0] == DATA_ROWS
    vmem = pl.BlockSpec(memory_space=pltpu.VMEM)
    sems = pltpu.SemaphoreType.DMA((len(plan.streams), plan.copies))
    return pl.pallas_call(
        functools.partial(sum_kernel, plan),
        out_shape=(
            jax.ShapeDtypeStruct(data.shape, jnp.float32),
            jax.ShapeDtypeStruct((3 * SLABS * F, LANES), jnp.float32),
            jax.ShapeDtypeStruct((4, F, F), jnp.bfloat16),
            jax.ShapeDtypeStruct((4, F, F), jnp.bfloat16),
        ),
        in_specs=[vmem],
        out_specs=(vmem,) * 4,
        scratch_shapes=[
            pltpu.VMEM((plan.held, LANES), jnp.float32),
            pltpu.VMEM((2, F, F), jnp.float32),
            pltpu.VMEM((2, LANES, LANES), jnp.float32),
            sems,
            sems,
            pltpu.SemaphoreType.DMA((4,)),
            pltpu.SemaphoreType.DMA((4,)),
        ],
        compiler_params=pltpu.CompilerParams(
            collective_id=1, has_side_effects=True, vmem_limit_bytes=60 * 2**20
        ),
        name="sum_and_invert",
    )(data)


def dot(a, b):
    return jnp.dot(a, b, preferred_element_type=jnp.float32)


def sweep_kernel(sum_ref, cross_ref, ih, il, ft_ref, y_ref, coef_ref, res_ref, gh, gl):
    core = lax.axis_index("blk")
    for own, (gref, base) in enumerate(((sum_ref, CROSS), (cross_ref, 0))):
        owner = core if own == 0 else 1 - core
        for k in range(3):
            for j in range(SLABS):
                high, low = split(gref[pl.ds(base + (k * SLABS + j) * F, F), :])
                cols = slice(j * LANES, (j + 1) * LANES)
                gh[3 * owner + k, :, cols] = high
                gl[3 * owner + k, :, cols] = low
    where = {(1, 0): 0, (2, 0): 1, (3, 1): 2, (3, 2): 3, (2, 1): 4, (3, 0): 5}

    def one(half, _):
        cols = pl.ds(pl.multiple_of(half * 256, 256), 256)
        rounded = []
        for b in range(4):
            corr = jnp.concatenate(
                [
                    sum_ref[pl.ds(pl.multiple_of(MOMENT + (b * SLABS + 2 * half + k) * F, F), F), :]
                    for k in range(2)
                ],
                axis=1,
            )
            for j in range(b):
                corr = corr - (dot(gh[where[b, j]], rounded[j]) + dot(gl[where[b, j]], rounded[j]))
            ch, cl = split(corr)
            delta = dot(ih[b], ch) + (dot(ih[b], cl) + dot(il[b], ch))
            coef_ref[b, :, cols] = delta
            rounded.append(delta.astype(jnp.bfloat16))
        fit = lax.dot_general(
            ft_ref[0], rounded[0], (((0,), (0,)), ((), ())), preferred_element_type=jnp.float32
        )
        for b in range(1, 4):
            fit = fit + lax.dot_general(
                ft_ref[b], rounded[b], (((0,), (0,)), ((), ())), preferred_element_type=jnp.float32
            )
        res_ref[:, cols] = y_ref[:, cols].astype(jnp.float32) - fit
        return 0

    lax.fori_loop(0, 2, one, 0)


def sweep(summed, cross, high, low, ft, y):
    vmem = pl.BlockSpec(memory_space=pltpu.VMEM)
    return pl.pallas_call(
        sweep_kernel,
        out_shape=(
            jax.ShapeDtypeStruct((4, F, y.shape[1]), jnp.float32),
            jax.ShapeDtypeStruct(y.shape, jnp.float32),
        ),
        in_specs=[vmem] * 6,
        out_specs=(vmem, vmem),
        scratch_shapes=[pltpu.VMEM((6, F, F), jnp.bfloat16), pltpu.VMEM((6, F, F), jnp.bfloat16)],
        compiler_params=pltpu.CompilerParams(vmem_limit_bytes=60 * 2**20),
        name="sweep",
    )(summed, cross, high, low, ft, y)


def body(inputs, proj, phase, targets):
    ft, parts = features_and_parts(jnp.swapaxes(inputs, 0, 1), proj, phase, targets)
    return sweep(*sum_and_invert(parts), ft, targets)


def solution(mesh):
    return jax.shard_map(
        body,
        mesh=mesh,
        in_specs=(P("rows", None), P("blk", None, None), P("blk", None), P("rows", "blk")),
        out_specs=(P(None, None, "blk"), P("rows", "blk")),
        check_vma=False,
    )
```

time: 1300 us -> 183 us (0.14)
  waiting for transfers between devices: 798 us -> 0 us
  other arithmetic: 337 us -> 0 us
  Pallas kernels: 0 us -> 182 us
  matrix products: 80.9 us -> 0 us
  local copies, waits for them, and re-layouts: 52.2 us -> 0 us
  between operations: 20.5 us -> 0.65 us
    psum x5 -> x0, waiting for transfers between devices: 776 us -> none  [the longest x4 736 us: body(): corr = lax.psum(partial_corr, 'rows')]
    another operation x44 -> x0, other arithmetic: 332 us -> none  [the longest x6 163 us: body(): delta = jax.scipy.linalg.cho_solve((factor, True), corr)]
    pallas_call x0 -> x3, Pallas kernels: none -> 182 us  [the longest x1 137 us: sum_and_invert(): pl.pallas_call(functools.partial(sum_kernel, plan), out_shape=(jax.ShapeD...]
    another operation x68 -> x0, matrix products: 45.3 us -> none  [the longest x56 34.4 us: body(): delta = jax.scipy.linalg.cho_solve((factor, True), corr)]
    another operation x61 -> x0, local copies, waits for them, and re-layouts: 42.7 us -> none  [the longest x53 42.4 us: body(): delta = jax.scipy.linalg.cho_solve((factor, True), corr)]
    dot_general x12 -> x0, matrix products: 35.5 us -> none  [the longest x2 19.5 us: build(): jnp.dot(inputs, weights, preferred_element_type=jnp.float32)]
    all_gather x1 -> x0, waiting for transfers between devices: 21.8 us -> none  [body(): factors = lax.all_gather(own_factors, 'blk', axis=0, tiled=True)]
  transfers between devices with their start and end apart: 6 -> 0, of which waited for: 6 -> 0; matrix products, arithmetic and copies ran while one was open for 13% -> 0% of each run, Pallas kernels for 0% -> 0%
where the time goes in v2:
time: 183 us
  Pallas kernels  182 us (99%)
    pallas_call x1, Pallas kernels, sum_and_invert(): pl.pallas_call(functools.partial(sum_kernel, plan), out_shape=(jax.ShapeD...  137 us
    pallas_call x1, Pallas kernels, sweep(): pl.pallas_call(sweep_kernel, out_shape=(jax.ShapeDtypeStruct((4, F, y.sha...  22.7 us
    pallas_call x1, Pallas kernels, features_and_parts(): pl.pallas_call(functools.partial(feature_kernel, scale), out_shape=(jax.S...  22.2 us

profile of v2, /device:TPU:1, one launch (start us, length us, event | category | flops | bytes accessed | tf_op | source)
XLA Modules:
  0.0 182.7 jit_solution(13780093181284705716)
XLA Ops:
  0.6 22.2 %features.1 = (bf16[4,512,1024]{2,1,0:T(8,128)(2,1)}, f32[16896,128]{1,0:T(8,128)}) custom-call(bf16[440,1024]{1,0:T(8,128)(2,1)} %bitcast.1, bf16[2,440,512]{2,1,0:T(8,128)(2,1)} %proj_ref.1, bf16[2,512]{1,0:T(2,128)(2,1)} %phase_ref.1, bf16[1024,512]{1,0:T(8,128)(2,1)} %y_ref.3), custom_call_target="tpu_custom_call" | custom-call | tf_op jit(solution)/shard_map/features/pallas_call | solution.py:155
  22.9 137.1 %sum_and_invert.1 = (f32[16896,128]{1,0:T(8,128)}, f32[6144,128]{1,0:T(8,128)}, bf16[4,512,512]{2,1,0:T(8,128)(2,1)}, bf16[4,512,512]{2,1,0:T(8,128)(2,1)}) custom-call(f32[16896,128]{1,0:T(8,128)} %get-tuple-element.8.data_ref), custom_call_target="tpu_custom_call" | custom-call | tf_op jit(solution)/shard_map/sum_and_invert/pallas_call | solution.py:587
  160.0 22.7 %sweep.1 = (f32[4,512,512]{2,1,0:T(8,128)}, f32[1024,512]{1,0:T(8,128)}) custom-call(f32[16896,128]{1,0:T(8,128)} %get-tuple-element.9.sum_ref, f32[6144,128]{1,0:T(8,128)} %get-tuple-element.10.cross_ref, bf16[4,512,512]{2,1,0:T(8,128)(2,1)} %get-tuple-element.11.ih, bf16[4,512,512]{2,1,0:T(8,128)(2,1)} %get-tuple-element.12.il, ...), custom_call_target="tpu_custom_call" | custom-call | tf_op jit(solution)/shard_map/sweep/pallas_call | solution.py:661

commit v3 on v2

--- a/solution.py
+++ b/solution.py
@@ -53,119 +53,108 @@
 SIN_POLY = fit_sin_poly()
 
 
-def feature_kernel(scale, xt_ref, proj_ref, phase_ref, y_ref, ft_ref, part_ref, send_sem, recv_sem):
-    core = lax.axis_index("blk")
-    rows = xt_ref.shape[1]
-    barrier = pltpu.get_barrier_semaphore()
-    pl.semaphore_signal(barrier, inc=1, device_id=sibling(), device_id_type=MESH)
-    pl.semaphore_wait(barrier, 1)
-
-    chunk = 256
-    copies = []
-    for i in range(2):
-        g = 2 * core + i
-        shift = jnp.broadcast_to(phase_ref[i:i + 1, :].astype(jnp.float32), (8, F)).T[:, :1]
-
-        def piece(j, _, i=i, g=g, shift=shift):
+class Parts:
+    def __init__(self, scale, xt_ref, proj_ref, phase_ref, y_ref, ft_ref, part_ref, send_sem, recv_sem):
+        self.scale, self.xt, self.proj, self.phase, self.y = scale, xt_ref, proj_ref, phase_ref, y_ref
+        self.ft, self.part, self.send_sem, self.recv_sem = ft_ref, part_ref, send_sem, recv_sem
+        self.core = lax.axis_index("blk")
+        self.own = [2 * self.core, 2 * self.core + 1]
+        self.other = [2 * (1 - self.core), 2 * (1 - self.core) + 1]
+
+    def exchange(self, i, receive=False):
+        return pltpu.make_async_remote_copy(
+            src_ref=self.ft.at[self.own[i]],
+            dst_ref=self.ft.at[(self.other if receive else self.own)[i]],
+            send_sem=self.send_sem.at[i],
+            recv_sem=self.recv_sem.at[i],
+            device_id=sibling(),
+            device_id_type=MESH,
+        )
+
+    def features(self, i):
+        chunk = 256
+        shift = jnp.broadcast_to(self.phase[i:i + 1, :].astype(jnp.float32), (8, F)).T[:, :1]
+
+        def piece(j, _):
             cols = pl.ds(pl.multiple_of(j * chunk, chunk), chunk)
             pre = lax.dot_general(
-                proj_ref[i], xt_ref[:, cols], (((0,), (0,)), ((), ())), preferred_element_type=jnp.float32
+                self.proj[i], self.xt[:, cols], (((0,), (0,)), ((), ())), preferred_element_type=jnp.float32
             )
             turns = (pre + shift) * (0.5 / math.pi)
             turns = turns - jnp.round(turns)
-            ft_ref[g, :, cols] = (cos_turns(turns) * scale).astype(jnp.bfloat16)
+            self.ft[self.own[i], :, cols] = (cos_turns(turns) * self.scale).astype(jnp.bfloat16)
             return 0
 
-        lax.fori_loop(0, rows // chunk, piece, 0)
-        copy = pltpu.make_async_remote_copy(
-            src_ref=ft_ref.at[g],
-            dst_ref=ft_ref.at[g],
-            send_sem=send_sem.at[i],
-            recv_sem=recv_sem.at[i],
-            device_id=sibling(),
-            device_id_type=MESH,
-        )
-        copy.start()
-        copies.append(copy)
-
-    def put(base, half, value):
+        lax.fori_loop(0, self.xt.shape[1] // chunk, piece, 0)
+        self.exchange(i).start()
+
+    def put(self, base, half, value):
         for k in range(2):
             row = pl.multiple_of(base + (2 * half + k) * F, LANES)
-            part_ref[pl.ds(row, F), :] = value[:, k * LANES:(k + 1) * LANES]
-
-    def diagonal(m, a):
+            self.part[pl.ds(row, F), :] = value[:, k * LANES:(k + 1) * LANES]
+
+    def diagonal(self, m):
+        a = self.own[m]
         for half in range(2):
             top = 256 * half
             value = lax.dot_general(
-                ft_ref[a, top:, :], ft_ref[a, top:top + 256, :], (((1,), (1,)), ((), ())),
+                self.ft[a, top:, :], self.ft[a, top:top + 256, :], (((1,), (1,)), ((), ())),
                 preferred_element_type=jnp.float32,
             )
             for k in range(2):
                 j = 2 * half + k
                 for i in range(j, SLABS):
                     rows = slice(i * LANES - top, (i + 1) * LANES - top)
-                    part_ref[pl.ds(tile_row(m, i, j), LANES), :] = value[rows, k * LANES:(k + 1) * LANES]
-
-    def gram(q, a, b):
+                    self.part[pl.ds(tile_row(m, i, j), LANES), :] = value[rows, k * LANES:(k + 1) * LANES]
+
+    def gram(self, q, a, b):
         def one(half, _):
             cols = pl.ds(pl.multiple_of(half * 256, 256), 256)
-            put(CROSS + q * SLABS * F, half, lax.dot_general(
-                ft_ref[a], ft_ref[b, cols, :], (((1,), (1,)), ((), ())), preferred_element_type=jnp.float32
+            self.put(CROSS + q * SLABS * F, half, lax.dot_general(
+                self.ft[a], self.ft[b, cols, :], (((1,), (1,)), ((), ())), preferred_element_type=jnp.float32
             ))
             return 0
 
         lax.fori_loop(0, 2, one, 0)
 
-    def moment(b):
+    def moment(self, b):
         def one(half, _):
             cols = pl.ds(pl.multiple_of(half * 256, 256), 256)
-            put(MOMENT + b * SLABS * F, half, jnp.dot(ft_ref[b], y_ref[:, cols], preferred_element_type=jnp.float32))
+            self.put(MOMENT + b * SLABS * F, half, jnp.dot(
+                self.ft[b], self.y[:, cols], preferred_element_type=jnp.float32
+            ))
             return 0
 
         lax.fori_loop(0, 2, one, 0)
 
-    own = [2 * core, 2 * core + 1]
-    other = [2 * (1 - core), 2 * (1 - core) + 1]
-    diagonal(0, own[0])
-    diagonal(1, own[1])
-    gram(0, own[1], own[0])
-    moment(own[0])
-    moment(own[1])
-    for i in range(2):
-        pltpu.make_async_remote_copy(
-            src_ref=ft_ref.at[own[i]],
-            dst_ref=ft_ref.at[other[i]],
-            send_sem=send_sem.at[i],
-            recv_sem=recv_sem.at[i],
-            device_id=sibling(),
-            device_id_type=MESH,
-        ).wait_recv()
-    gram(1, 2, core)
-    gram(2, 3, 1 - core)
-    moment(other[0])
-    moment(other[1])
-    for copy in copies:
-        copy.wait_send()
-
-
-def features_and_parts(xt, proj, phase, y):
-    rows = xt.shape[1]
-    scale = 1.0 / math.sqrt(rows * 128)
-    vmem = pl.BlockSpec(memory_space=pltpu.VMEM)
-    return pl.pallas_call(
-        functools.partial(feature_kernel, scale),
-        out_shape=(
-            jax.ShapeDtypeStruct((4, F, rows), jnp.bfloat16),
-            jax.ShapeDtypeStruct((DATA_ROWS, LANES), jnp.float32),
-        ),
-        in_specs=[vmem] * 4,
-        out_specs=(vmem, vmem),
-        scratch_shapes=[pltpu.SemaphoreType.DMA((2,)), pltpu.SemaphoreType.DMA((2,))],
-        compiler_params=pltpu.CompilerParams(
-            collective_id=0, has_side_effects=True, vmem_limit_bytes=60 * 2**20
-        ),
-        name="features",
-    )(xt, proj, phase, y)
+    def first(self):
+        for i in range(2):
+            self.features(i)
+        for i in range(2):
+            self.diagonal(i)
+        self.gram(0, self.own[1], self.own[0])
+
+    @staticmethod
+    def durations():
+        return [1.0] * 6
+
+    def rest(self):
+        yield functools.partial(self.moment, self.own[0])
+        yield functools.partial(self.moment, self.own[1])
+
+        def crossed():
+            for i in range(2):
+                self.exchange(i, receive=True).wait_recv()
+            self.gram(1, 2, self.core)
+
+        yield crossed
+        yield functools.partial(self.gram, 2, 3, 1 - self.core)
+        yield functools.partial(self.moment, self.other[0])
+        yield functools.partial(self.moment, self.other[1])
+
+    def finish(self):
+        for i in range(2):
+            self.exchange(i).wait_send()
 
 
 AXES = ((4, 32), (8, 4), (4, 1))
@@ -223,7 +212,7 @@
 
 
 class Plan:
-    def __init__(self, rounds, latency=2.4, rate=47e3, extra=()):
+    def __init__(self, rounds, latency=2.0, rate=47e3, extra=(), before=()):
         self.streams, held, base = [], 0, 0
         for number, (units, modes, delay) in enumerate(rounds):
             for part in range(3):
@@ -238,9 +227,9 @@
                     self.streams.append(st)
         self.held, self.rows = held, base
         self.copies = max(st.count for st in self.streams)
-        self.simulate(latency, rate, extra)
-
-    def simulate(self, latency, rate, extra=()):
+        self.simulate(latency, rate, extra, before)
+
+    def simulate(self, latency, rate, extra=(), before=()):
         free, order, ready, core = {}, [], [], 0.0
         arrival = {}
 
@@ -260,6 +249,7 @@
         nxt = {}
         for st in self.streams:
             nxt[st.index] = -1
+        early = list(before)
         pieces, done0 = list(extra), len([s for s in self.streams if s.round == 0])
         self.round_end = {}
         while True:
@@ -274,6 +264,10 @@
                     best = (key, st)
             if best is None:
                 break
+            if early and (best[0][0] > core + 0.3 or best[1].round > 0):
+                core += early.pop(0)
+                order.append(("early", None))
+                continue
             if pieces and done0 == 0 and best[0][0] > core + 0.3:
                 core += pieces.pop(0)
                 order.append(("piece", None))
@@ -519,8 +513,8 @@
                 work[m, rows, :] = work[m, rows, :] - mm(col[rows], full)
 
 
-def sum_kernel(plan, data_ref, out_ref, cross_ref, high_ref, low_ref, held, work, pivot,
-               send_sem, recv_sem, pair_send, pair_recv):
+def sum_kernel(plan, scale, xt_ref, proj_ref, phase_ref, y_ref, ft_ref, out_ref, cross_ref, high_ref, low_ref,
+               data_ref, held, work, pivot, send_sem, recv_sem, pair_send, pair_recv, feat_send, feat_recv):
     ring = Ring(plan, data_ref, out_ref, held, send_sem, recv_sem)
     core = lax.axis_index("blk")
     other = 2 * ring.r + 1 - core
@@ -542,16 +536,21 @@
         start, rows = ((0, SLABS * F), (SLABS * F, 2 * SLABS * F))[slot]
         return pair(slot, out_ref.at[pl.ds(CROSS + start, rows), :], cross_ref.at[pl.ds(start, rows), :])
 
+    parts = Parts(scale, xt_ref, proj_ref, phase_ref, y_ref, ft_ref, data_ref, feat_send, feat_recv)
+    parts.first()
+    early = parts.rest()
     inverses = Inverses(out_ref, work, pivot)
     pieces = inverses.pieces()
-    left = [sum(st.round == n for st in plan.streams) for n in range(3)]
+    left = [sum(st.round == n for st in plan.streams) for n in range(2)]
     for what, arg in plan.order:
         if what == "piece":
             next(pieces)()
+        elif what == "early":
+            next(early)()
         elif what == "end":
             n = plan.streams[arg].round
             left[n] -= 1
-            if n < 2 and left[n] == 0:
+            if left[n] == 0:
                 cross(n).start()
         else:
             ring.event(what, arg)
@@ -562,6 +561,7 @@
     for k, ref in enumerate((high_ref, low_ref)):
         pair(2 + k, ref.at[pl.ds(2 * core, 2)], ref.at[pl.ds(2 * core, 2)]).start()
     ring.finish()
+    parts.finish()
     for slot in range(2):
         cross(slot).wait()
     for k, ref in enumerate((high_ref, low_ref)):
@@ -569,32 +569,35 @@
 
 
 def mode(first, second, middle):
-    return ((first, second, "direct"), (middle, second), (first, second, "direct"))
+    return ((first, second, "direct"), (middle, "direct"), (first, second, "direct"))
 
 
 ROUNDS = (
     ((1024, 256, 1024), mode("ring", "direct", "ring"), 0.0),
-    ((1024, 1024, 1024), mode("ring", "ring", "ring"), 1.0),
-    ((1024, 1024, 1024), mode("ring", "ring", "ring"), 2.0),
+    ((2048, 2048, 2048), mode("ring", "ring", "ring"), 7.0),
 )
 
 
-def sum_and_invert(data):
-    plan = Plan(ROUNDS, extra=Inverses.durations())
-    assert plan.rows == data.shape[0] == DATA_ROWS
+def sum_and_invert(xt, proj, phase, y):
+    rows = xt.shape[1]
+    scale = 1.0 / math.sqrt(rows * 128)
+    plan = Plan(ROUNDS, extra=Inverses.durations(), before=Parts.durations())
+    assert plan.rows == DATA_ROWS
     vmem = pl.BlockSpec(memory_space=pltpu.VMEM)
     sems = pltpu.SemaphoreType.DMA((len(plan.streams), plan.copies))
     return pl.pallas_call(
-        functools.partial(sum_kernel, plan),
+        functools.partial(sum_kernel, plan, scale),
         out_shape=(
-            jax.ShapeDtypeStruct(data.shape, jnp.float32),
+            jax.ShapeDtypeStruct((4, F, rows), jnp.bfloat16),
+            jax.ShapeDtypeStruct((DATA_ROWS, LANES), jnp.float32),
             jax.ShapeDtypeStruct((3 * SLABS * F, LANES), jnp.float32),
             jax.ShapeDtypeStruct((4, F, F), jnp.bfloat16),
             jax.ShapeDtypeStruct((4, F, F), jnp.bfloat16),
         ),
-        in_specs=[vmem],
-        out_specs=(vmem,) * 4,
+        in_specs=[vmem] * 4,
+        out_specs=(vmem,) * 5,
         scratch_shapes=[
+            pltpu.VMEM((DATA_ROWS, LANES), jnp.float32),
             pltpu.VMEM((plan.held, LANES), jnp.float32),
             pltpu.VMEM((2, F, F), jnp.float32),
             pltpu.VMEM((2, LANES, LANES), jnp.float32),
@@ -602,79 +605,126 @@
             sems,
             pltpu.SemaphoreType.DMA((4,)),
             pltpu.SemaphoreType.DMA((4,)),
+            pltpu.SemaphoreType.DMA((2,)),
+            pltpu.SemaphoreType.DMA((2,)),
         ],
         compiler_params=pltpu.CompilerParams(
             collective_id=1, has_side_effects=True, vmem_limit_bytes=60 * 2**20
         ),
         name="sum_and_invert",
-    )(data)
+    )(xt, proj, phase, y)
 
 
 def dot(a, b):
     return jnp.dot(a, b, preferred_element_type=jnp.float32)
 
 
-def sweep_kernel(sum_ref, cross_ref, ih, il, ft_ref, y_ref, coef_ref, res_ref, gh, gl):
+def sweep_kernel(sum_hbm, cross_hbm, ih_hbm, il_hbm, ft_hbm, y_ref, coef_ref, res_ref,
+                 own_g, other_g, moments, ih, il, ft, gh, gl, sems):
     core = lax.axis_index("blk")
-    for own, (gref, base) in enumerate(((sum_ref, CROSS), (cross_ref, 0))):
-        owner = core if own == 0 else 1 - core
-        for k in range(3):
-            for j in range(SLABS):
-                high, low = split(gref[pl.ds(base + (k * SLABS + j) * F, F), :])
-                cols = slice(j * LANES, (j + 1) * LANES)
-                gh[3 * owner + k, :, cols] = high
-                gl[3 * owner + k, :, cols] = low
+    half = pl.program_id(0)
+    block = SLABS * F
+    loads = {}
+
+    def load(name, src, dst):
+        loads[name] = pltpu.make_async_copy(src, dst, sems.at[len(loads)])
+
+    for b in range(4):
+        load(("high", b), ih_hbm.at[b], ih.at[b])
+        load(("low", b), il_hbm.at[b], il.at[b])
+        rows = pl.ds(b * block, block)
+        load(("moment", b), sum_hbm.at[pl.ds(MOMENT + b * block, block), :], moments.at[rows, :])
+        if b == 0:
+            load(("own", 0), sum_hbm.at[pl.ds(CROSS, 3 * block), :], own_g)
+            load(("other", 0), cross_hbm, other_g)
+    for b in range(4):
+        load(("ft", b), ft_hbm.at[b], ft.at[b])
+
+    def wait(*names):
+        @pl.when(half == 0)
+        def _():
+            for name in names:
+                loads[name].wait()
+
+    @pl.when(half == 0)
+    def _():
+        for copy in loads.values():
+            copy.start()
+
     where = {(1, 0): 0, (2, 0): 1, (3, 1): 2, (3, 2): 3, (2, 1): 4, (3, 0): 5}
-
-    def one(half, _):
-        cols = pl.ds(pl.multiple_of(half * 256, 256), 256)
-        rounded = []
-        for b in range(4):
-            corr = jnp.concatenate(
-                [
-                    sum_ref[pl.ds(pl.multiple_of(MOMENT + (b * SLABS + 2 * half + k) * F, F), F), :]
-                    for k in range(2)
-                ],
-                axis=1,
-            )
-            for j in range(b):
-                corr = corr - (dot(gh[where[b, j]], rounded[j]) + dot(gl[where[b, j]], rounded[j]))
-            ch, cl = split(corr)
-            delta = dot(ih[b], ch) + (dot(ih[b], cl) + dot(il[b], ch))
-            coef_ref[b, :, cols] = delta
-            rounded.append(delta.astype(jnp.bfloat16))
-        fit = lax.dot_general(
-            ft_ref[0], rounded[0], (((0,), (0,)), ((), ())), preferred_element_type=jnp.float32
+    rounded = []
+    for b in range(4):
+        wait(("high", b), ("low", b), ("moment", b))
+        if b == 1:
+            wait(("own", 0), ("other", 0))
+
+            @pl.when(half == 0)
+            def _():
+                for gref, owner in ((own_g, core), (other_g, 1 - core)):
+                    for k in range(3):
+                        for j in range(SLABS):
+                            high, low = split(gref[pl.ds((k * SLABS + j) * F, F), :])
+                            cols = slice(j * LANES, (j + 1) * LANES)
+                            gh[3 * owner + k, :, cols] = high
+                            gl[3 * owner + k, :, cols] = low
+
+        corr = jnp.concatenate(
+            [
+                moments[pl.ds(pl.multiple_of((b * SLABS + 2 * half + k) * F, F), F), :]
+                for k in range(2)
+            ],
+            axis=1,
         )
-        for b in range(1, 4):
-            fit = fit + lax.dot_general(
-                ft_ref[b], rounded[b], (((0,), (0,)), ((), ())), preferred_element_type=jnp.float32
-            )
-        res_ref[:, cols] = y_ref[:, cols].astype(jnp.float32) - fit
-        return 0
-
-    lax.fori_loop(0, 2, one, 0)
-
-
-def sweep(summed, cross, high, low, ft, y):
-    vmem = pl.BlockSpec(memory_space=pltpu.VMEM)
+        for j in range(b):
+            corr = corr - (dot(gh[where[b, j]], rounded[j]) + dot(gl[where[b, j]], rounded[j]))
+        ch, cl = split(corr)
+        delta = dot(ih[b], ch) + (dot(ih[b], cl) + dot(il[b], ch))
+        coef_ref[b] = delta
+        rounded.append(delta.astype(jnp.bfloat16))
+    fit = None
+    for b in range(4):
+        wait(("ft", b))
+        term = lax.dot_general(
+            ft[b], rounded[b], (((0,), (0,)), ((), ())), preferred_element_type=jnp.float32
+        )
+        fit = term if fit is None else fit + term
+    res_ref[...] = y_ref[...].astype(jnp.float32) - fit
+
+
+def sweep(ft, summed, cross, high, low, y):
+    rows, cols = y.shape
+    any_space = pl.BlockSpec(memory_space=pl.ANY)
     return pl.pallas_call(
         sweep_kernel,
+        grid=(2,),
         out_shape=(
-            jax.ShapeDtypeStruct((4, F, y.shape[1]), jnp.float32),
+            jax.ShapeDtypeStruct((4, F, cols), jnp.float32),
             jax.ShapeDtypeStruct(y.shape, jnp.float32),
         ),
-        in_specs=[vmem] * 6,
-        out_specs=(vmem, vmem),
-        scratch_shapes=[pltpu.VMEM((6, F, F), jnp.bfloat16), pltpu.VMEM((6, F, F), jnp.bfloat16)],
+        in_specs=[any_space] * 5 + [pl.BlockSpec((rows, cols // 2), lambda i: (0, i))],
+        out_specs=(
+            pl.BlockSpec((4, F, cols // 2), lambda i: (0, 0, i)),
+            pl.BlockSpec((rows, cols // 2), lambda i: (0, i)),
+        ),
+        scratch_shapes=[
+            pltpu.VMEM((3 * SLABS * F, LANES), jnp.float32),
+            pltpu.VMEM((3 * SLABS * F, LANES), jnp.float32),
+            pltpu.VMEM((4 * SLABS * F, LANES), jnp.float32),
+            pltpu.VMEM((4, F, F), jnp.bfloat16),
+            pltpu.VMEM((4, F, F), jnp.bfloat16),
+            pltpu.VMEM((4, F, rows), jnp.bfloat16),
+            pltpu.VMEM((6, F, F), jnp.bfloat16),
+            pltpu.VMEM((6, F, F), jnp.bfloat16),
+            pltpu.SemaphoreType.DMA((18,)),
+        ],
         compiler_params=pltpu.CompilerParams(vmem_limit_bytes=60 * 2**20),
         name="sweep",
     )(summed, cross, high, low, ft, y)
 
 
 def body(inputs, proj, phase, targets):
-    ft, parts = features_and_parts(jnp.swapaxes(inputs, 0, 1), proj, phase, targets)
-    return sweep(*sum_and_invert(parts), ft, targets)
+    ft, summed, cross, high, low = sum_and_invert(jnp.swapaxes(inputs, 0, 1), proj, phase, targets)
+    return sweep(ft, summed, cross, high, low, targets)
 
 
 def solution(mesh):

time: 183 us -> 173 us (0.945)
  Pallas kernels: 182 us -> 172 us
    pallas_call x3 -> x2, Pallas kernels: 182 us -> 172 us  [the longest x1 147 us: sum_and_invert(): pl.pallas_call(functools.partial(sum_kernel, plan, scale), out_shape=(jax...]
where the time goes in v3:
time: 173 us
  Pallas kernels  172 us (99%)
    pallas_call x1, Pallas kernels, sum_and_invert(): pl.pallas_call(functools.partial(sum_kernel, plan, scale), out_shape=(jax...  147 us
    pallas_call x1, Pallas kernels, sweep(): pl.pallas_call(sweep_kernel, grid=(2,), out_shape=(jax.ShapeDtypeStruct((...  24.9 us

profile of v3, /device:TPU:1, one launch (start us, length us, event | category | flops | bytes accessed | tf_op | source)
XLA Modules:
  0.0 172.9 jit_solution(1733127659290197125)
XLA Ops:
  0.6 147.2 %sum_and_invert.1 = (bf16[4,512,1024]{2,1,0:T(8,128)(2,1)}, f32[16896,128]{1,0:T(8,128)}, f32[6144,128]{1,0:T(8,128)}, bf16[4,512,512]{2,1,0:T(8,128)(2,1)}, bf16[4,512,512]{2,1,0:T(8,128)(2,1)}) custom-call(bf16[440,1024]{1,0:T(8,128)(2,1)} %bitcast.1, bf16[2,440,512]{2,1,0:T(8,128)(2,1)} %proj_ref.1, bf16[2,512]{1,0:T(2,128)(2,1)} %phase_ref.1, ...), custom_call_target="tpu_custom_call" | custom-call | tf_op jit(solution)/shard_map/sum_and_invert/pallas_call | solution.py:588
  147.8 24.9 %sweep.1 = (f32[4,512,512]{2,1,0:T(8,128)}, f32[1024,512]{1,0:T(8,128)}) custom-call(f32[16896,128]{1,0:T(8,128)} %get-tuple-element.7.sum_hbm, f32[6144,128]{1,0:T(8,128)} %get-tuple-element.8.cross_hbm, bf16[4,512,512]{2,1,0:T(8,128)(2,1)} %get-tuple-element.9.ih_hbm, bf16[4,512,512]{2,1,0:T(8,128)(2,1)} %get-tuple-element.10.il_hbm, ...), custom_call_target="tpu_custom_call" | custom-call | tf_op jit(solution)/shard_map/sweep/pallas_call | solution.py:697

commit v4 on v3

--- a/solution.py
+++ b/solution.py
@@ -169,7 +169,7 @@
 
 class Stream:
     def __init__(self, index, part, direction, base, length, held, modes):
-        self.index, self.dir, self.base = index, direction, base
+        self.index, self.dir, self.base, self.length = index, direction, base, length
         self.order, last = PARTS[part]
         depth = len(self.order)
         self.rows = []
@@ -513,8 +513,9 @@
                 work[m, rows, :] = work[m, rows, :] - mm(col[rows], full)
 
 
-def sum_kernel(plan, scale, xt_ref, proj_ref, phase_ref, y_ref, ft_ref, out_ref, cross_ref, high_ref, low_ref,
-               data_ref, held, work, pivot, send_sem, recv_sem, pair_send, pair_recv, feat_send, feat_recv):
+def sum_kernel(plan, scale, xt_ref, proj_ref, phase_ref, y_ref, ft_hbm, sum_hbm, cross_hbm, high_hbm, low_hbm,
+               ft_ref, out_ref, high_ref, low_ref, data_ref, held, work, pivot,
+               send_sem, recv_sem, pair_send, pair_recv, feat_send, feat_recv, store_sem):
     ring = Ring(plan, data_ref, out_ref, held, send_sem, recv_sem)
     core = lax.axis_index("blk")
     other = 2 * ring.r + 1 - core
@@ -532,40 +533,56 @@
             device_id=other, device_id_type=LOGICAL,
         )
 
+    crossing = [st for st in plan.streams if CROSS <= st.base and st.base + st.length <= MOMENT]
+    assert sum(st.length for st in crossing) == MOMENT - CROSS and len(crossing) == 4
+
     def cross(slot):
-        start, rows = ((0, SLABS * F), (SLABS * F, 2 * SLABS * F))[slot]
-        return pair(slot, out_ref.at[pl.ds(CROSS + start, rows), :], cross_ref.at[pl.ds(start, rows), :])
+        st = crossing[slot]
+        rows = st.length
+        return pair(2 + slot, out_ref.at[pl.ds(st.base, rows), :], cross_hbm.at[pl.ds(st.base - CROSS, rows), :])
+
+    stores = []
+
+    def store(src, dst):
+        stores.append(pltpu.make_async_copy(src, dst, store_sem.at[len(stores)]))
+        stores[-1].start()
 
     parts = Parts(scale, xt_ref, proj_ref, phase_ref, y_ref, ft_ref, data_ref, feat_send, feat_recv)
     parts.first()
+    for i in range(2):
+        store(ft_ref.at[parts.own[i]], ft_hbm.at[parts.own[i]])
     early = parts.rest()
     inverses = Inverses(out_ref, work, pivot)
     pieces = inverses.pieces()
-    left = [sum(st.round == n for st in plan.streams) for n in range(2)]
     for what, arg in plan.order:
         if what == "piece":
             next(pieces)()
         elif what == "early":
             next(early)()
         elif what == "end":
-            n = plan.streams[arg].round
-            left[n] -= 1
-            if left[n] == 0:
-                cross(n).start()
+            st = plan.streams[arg]
+            rows = pl.ds(st.base, st.length)
+            store(out_ref.at[rows, :], sum_hbm.at[rows, :])
+            if st in crossing:
+                cross(crossing.index(st)).start()
         else:
             ring.event(what, arg)
+    for i in range(2):
+        store(ft_ref.at[parts.other[i]], ft_hbm.at[parts.other[i]])
+    mine, theirs = pl.ds(2 * core, 2), pl.ds(2 * (1 - core), 2)
     for m in range(2):
-        high, low = split(work[m])
-        high_ref[2 * core + m] = high
-        low_ref[2 * core + m] = low
-    for k, ref in enumerate((high_ref, low_ref)):
-        pair(2 + k, ref.at[pl.ds(2 * core, 2)], ref.at[pl.ds(2 * core, 2)]).start()
+        high_ref[m], low_ref[m] = split(work[m])
+    for k, (ref, dst) in enumerate(((high_ref, high_hbm), (low_ref, low_hbm))):
+        pair(k, ref, dst.at[mine]).start()
+        store(ref, dst.at[mine])
     ring.finish()
     parts.finish()
-    for slot in range(2):
+    for slot in range(len(crossing)):
         cross(slot).wait()
-    for k, ref in enumerate((high_ref, low_ref)):
-        pair(2 + k, ref.at[pl.ds(2 * core, 2)], ref.at[pl.ds(2 * (1 - core), 2)]).wait()
+    for k, (ref, dst) in enumerate(((high_ref, high_hbm), (low_ref, low_hbm))):
+        pair(k, ref, dst.at[theirs]).wait()
+    for copy in stores:
+        copy.wait()
 
 
 def mode(first, second, middle):
@@ -595,18 +612,23 @@
             jax.ShapeDtypeStruct((4, F, F), jnp.bfloat16),
         ),
         in_specs=[vmem] * 4,
-        out_specs=(vmem,) * 5,
+        out_specs=(pl.BlockSpec(memory_space=pl.ANY),) * 5,
         scratch_shapes=[
+            pltpu.VMEM((4, F, rows), jnp.bfloat16),
+            pltpu.VMEM((DATA_ROWS, LANES), jnp.float32),
+            pltpu.VMEM((2, F, F), jnp.bfloat16),
+            pltpu.VMEM((2, F, F), jnp.bfloat16),
             pltpu.VMEM((DATA_ROWS, LANES), jnp.float32),
             pltpu.VMEM((plan.held, LANES), jnp.float32),
             pltpu.VMEM((2, F, F), jnp.float32),
             pltpu.VMEM((2, LANES, LANES), jnp.float32),
             sems,
             sems,
-            pltpu.SemaphoreType.DMA((4,)),
-            pltpu.SemaphoreType.DMA((4,)),
+            pltpu.SemaphoreType.DMA((6,)),
+            pltpu.SemaphoreType.DMA((6,)),
             pltpu.SemaphoreType.DMA((2,)),
             pltpu.SemaphoreType.DMA((2,)),
+            pltpu.SemaphoreType.DMA((len(plan.streams) + 6,)),
         ],
         compiler_params=pltpu.CompilerParams(
             collective_id=1, has_side_effects=True, vmem_limit_bytes=60 * 2**20
@@ -619,104 +641,59 @@
     return jnp.dot(a, b, preferred_element_type=jnp.float32)
 
 
-def sweep_kernel(sum_hbm, cross_hbm, ih_hbm, il_hbm, ft_hbm, y_ref, coef_ref, res_ref,
-                 own_g, other_g, moments, ih, il, ft, gh, gl, sems):
+def sweep_kernel(sum_ref, cross_ref, ih, il, ft_ref, y_ref, coef_ref, res_ref, gh, gl):
     core = lax.axis_index("blk")
-    half = pl.program_id(0)
-    block = SLABS * F
-    loads = {}
-
-    def load(name, src, dst):
-        loads[name] = pltpu.make_async_copy(src, dst, sems.at[len(loads)])
-
-    for b in range(4):
-        load(("high", b), ih_hbm.at[b], ih.at[b])
-        load(("low", b), il_hbm.at[b], il.at[b])
-        rows = pl.ds(b * block, block)
-        load(("moment", b), sum_hbm.at[pl.ds(MOMENT + b * block, block), :], moments.at[rows, :])
-        if b == 0:
-            load(("own", 0), sum_hbm.at[pl.ds(CROSS, 3 * block), :], own_g)
-            load(("other", 0), cross_hbm, other_g)
-    for b in range(4):
-        load(("ft", b), ft_hbm.at[b], ft.at[b])
-
-    def wait(*names):
-        @pl.when(half == 0)
-        def _():
-            for name in names:
-                loads[name].wait()
-
-    @pl.when(half == 0)
-    def _():
-        for copy in loads.values():
-            copy.start()
-
+    for own, (gref, base) in enumerate(((sum_ref, CROSS), (cross_ref, 0))):
+        owner = core if own == 0 else 1 - core
+        for k in range(3):
+            for j in range(SLABS):
+                high, low = split(gref[pl.ds(base + (k * SLABS + j) * F, F), :])
+                cols = slice(j * LANES, (j + 1) * LANES)
+                gh[3 * owner + k, :, cols] = high
+                gl[3 * owner + k, :, cols] = low
     where = {(1, 0): 0, (2, 0): 1, (3, 1): 2, (3, 2): 3, (2, 1): 4, (3, 0): 5}
-    rounded = []
-    for b in range(4):
-        wait(("high", b), ("low", b), ("moment", b))
-        if b == 1:
-            wait(("own", 0), ("other", 0))
-
-            @pl.when(half == 0)
-            def _():
-                for gref, owner in ((own_g, core), (other_g, 1 - core)):
-                    for k in range(3):
-                        for j in range(SLABS):
-                            high, low = split(gref[pl.ds((k * SLABS + j) * F, F), :])
-                            cols = slice(j * LANES, (j + 1) * LANES)
-                            gh[3 * owner + k, :, cols] = high
-                            gl[3 * owner + k, :, cols] = low
-
-        corr = jnp.concatenate(
-            [
-                moments[pl.ds(pl.multiple_of((b * SLABS + 2 * half + k) * F, F), F), :]
-                for k in range(2)
-            ],
-            axis=1,
+
+    def one(half, _):
+        cols = pl.ds(pl.multiple_of(half * 256, 256), 256)
+        rounded = []
+        for b in range(4):
+            corr = jnp.concatenate(
+                [
+                    sum_ref[pl.ds(pl.multiple_of(MOMENT + (b * SLABS + 2 * half + k) * F, F), F), :]
+                    for k in range(2)
+                ],
+                axis=1,
+            )
+            for j in range(b):
+                corr = corr - (dot(gh[where[b, j]], rounded[j]) + dot(gl[where[b, j]], rounded[j]))
+            ch, cl = split(corr)
+            delta = dot(ih[b], ch) + (dot(ih[b], cl) + dot(il[b], ch))
+            coef_ref[b, :, cols] = delta
+            rounded.append(delta.astype(jnp.bfloat16))
+        fit = lax.dot_general(
+            ft_ref[0], rounded[0], (((0,), (0,)), ((), ())), preferred_element_type=jnp.float32
         )
-        for j in range(b):
-            corr = corr - (dot(gh[where[b, j]], rounded[j]) + dot(gl[where[b, j]], rounded[j]))
-        ch, cl = split(corr)
-        delta = dot(ih[b], ch) + (dot(ih[b], cl) + dot(il[b], ch))
-        coef_ref[b] = delta
-        rounded.append(delta.astype(jnp.bfloat16))
-    fit = None
-    for b in range(4):
-        wait(("ft", b))
-        term = lax.dot_general(
-            ft[b], rounded[b], (((0,), (0,)), ((), ())), preferred_element_type=jnp.float32
-        )
-        fit = term if fit is None else fit + term
-    res_ref[...] = y_ref[...].astype(jnp.float32) - fit
-
-
-def sweep(ft, summed, cross, high, low, y):
-    rows, cols = y.shape
-    any_space = pl.BlockSpec(memory_space=pl.ANY)
+        for b in range(1, 4):
+            fit = fit + lax.dot_general(
+                ft_ref[b], rounded[b], (((0,), (0,)), ((), ())), preferred_element_type=jnp.float32
+            )
+        res_ref[:, cols] = y_ref[:, cols].astype(jnp.float32) - fit
+        return 0
+
+    lax.fori_loop(0, 2, one, 0)
+
+
+def sweep(summed, cross, high, low, ft, y):
+    vmem = pl.BlockSpec(memory_space=pltpu.VMEM)
     return pl.pallas_call(
         sweep_kernel,
-        grid=(2,),
         out_shape=(
-            jax.ShapeDtypeStruct((4, F, cols), jnp.float32),
+            jax.ShapeDtypeStruct((4, F, y.shape[1]), jnp.float32),
             jax.ShapeDtypeStruct(y.shape, jnp.float32),
         ),
-        in_specs=[any_space] * 5 + [pl.BlockSpec((rows, cols // 2), lambda i: (0, i))],
-        out_specs=(
-            pl.BlockSpec((4, F, cols // 2), lambda i: (0, 0, i)),
-            pl.BlockSpec((rows, cols // 2), lambda i: (0, i)),
-        ),
-        scratch_shapes=[
-            pltpu.VMEM((3 * SLABS * F, LANES), jnp.float32),
-            pltpu.VMEM((3 * SLABS * F, LANES), jnp.float32),
-            pltpu.VMEM((4 * SLABS * F, LANES), jnp.float32),
-            pltpu.VMEM((4, F, F), jnp.bfloat16),
-            pltpu.VMEM((4, F, F), jnp.bfloat16),
-            pltpu.VMEM((4, F, rows), jnp.bfloat16),
-            pltpu.VMEM((6, F, F), jnp.bfloat16),
-            pltpu.VMEM((6, F, F), jnp.bfloat16),
-            pltpu.SemaphoreType.DMA((18,)),
-        ],
+        in_specs=[vmem] * 6,
+        out_specs=(vmem, vmem),
+        scratch_shapes=[pltpu.VMEM((6, F, F), jnp.bfloat16), pltpu.VMEM((6, F, F), jnp.bfloat16)],
         compiler_params=pltpu.CompilerParams(vmem_limit_bytes=60 * 2**20),
         name="sweep",
     )(summed, cross, high, low, ft, y)
@@ -724,7 +701,7 @@
 
 def body(inputs, proj, phase, targets):
     ft, summed, cross, high, low = sum_and_invert(jnp.swapaxes(inputs, 0, 1), proj, phase, targets)
-    return sweep(ft, summed, cross, high, low, targets)
+    return sweep(summed, cross, high, low, ft, targets)
 
 
 def solution(mesh):

time: 173 us -> 162 us (0.936)
  Pallas kernels: 172 us -> 161 us
    pallas_call x1, Pallas kernels: 147 us -> 138 us  [sum_and_invert(): pl.pallas_call(functools.partial(sum_kernel, plan, scale), out_shape=(jax...]
    pallas_call x1, Pallas kernels: 24.9 us -> 22.8 us  [sweep(): pl.pallas_call(sweep_kernel, out_shape=(jax.ShapeDtypeStruct((4, F, y.sha...]
where the time goes in v4:
time: 162 us
  Pallas kernels  161 us (99%)
    pallas_call x1, Pallas kernels, sum_and_invert(): pl.pallas_call(functools.partial(sum_kernel, plan, scale), out_shape=(jax...  138 us
    pallas_call x1, Pallas kernels, sweep(): pl.pallas_call(sweep_kernel, out_shape=(jax.ShapeDtypeStruct((4, F, y.sha...  22.8 us

profile of v4, /device:TPU:1, one launch (start us, length us, event | category | flops | bytes accessed | tf_op | source)
XLA Modules:
  0.0 161.8 jit_solution(5511222472748923317)
XLA Ops:
  0.6 138.4 %sum_and_invert.1 = (bf16[4,512,1024]{2,1,0:T(8,128)(2,1)}, f32[16896,128]{1,0:T(8,128)}, f32[6144,128]{1,0:T(8,128)}, bf16[4,512,512]{2,1,0:T(8,128)(2,1)}, bf16[4,512,512]{2,1,0:T(8,128)(2,1)}) custom-call(bf16[440,1024]{1,0:T(8,128)(2,1)} %bitcast.1, bf16[2,440,512]{2,1,0:T(8,128)(2,1)} %proj_ref.1, bf16[2,512]{1,0:T(2,128)(2,1)} %phase_ref.1, ...), custom_call_target="tpu_custom_call" | custom-call | tf_op jit(solution)/shard_map/sum_and_invert/pallas_call | solution.py:605
  139.1 22.8 %sweep.1 = (f32[4,512,512]{2,1,0:T(8,128)}, f32[1024,512]{1,0:T(8,128)}) custom-call(f32[16896,128]{1,0:T(8,128)} %get-tuple-element.7.sum_ref, f32[6144,128]{1,0:T(8,128)} %get-tuple-element.8.cross_ref, bf16[4,512,512]{2,1,0:T(8,128)(2,1)} %get-tuple-element.9.ih, bf16[4,512,512]{2,1,0:T(8,128)(2,1)} %get-tuple-element.10.il, ...), custom_call_target="tpu_custom_call" | custom-call | tf_op jit(solution)/shard_map/sweep/pallas_call | solution.py:688

commit v5 on v4

--- a/solution.py
+++ b/solution.py
@@ -212,7 +212,7 @@
 
 
 class Plan:
-    def __init__(self, rounds, latency=2.0, rate=47e3, extra=(), before=()):
+    def __init__(self, rounds, latency=2.4, rate=47e3, extra=(), before=()):
         self.streams, held, base = [], 0, 0
         for number, (units, modes, delay) in enumerate(rounds):
             for part in range(3):
@@ -643,56 +643,64 @@
 
 def sweep_kernel(sum_ref, cross_ref, ih, il, ft_ref, y_ref, coef_ref, res_ref, gh, gl):
     core = lax.axis_index("blk")
-    for own, (gref, base) in enumerate(((sum_ref, CROSS), (cross_ref, 0))):
-        owner = core if own == 0 else 1 - core
-        for k in range(3):
-            for j in range(SLABS):
-                high, low = split(gref[pl.ds(base + (k * SLABS + j) * F, F), :])
-                cols = slice(j * LANES, (j + 1) * LANES)
-                gh[3 * owner + k, :, cols] = high
-                gl[3 * owner + k, :, cols] = low
+    half = pl.program_id(0)
+
+    @pl.when(half == 0)
+    def _():
+        for own, (gref, base) in enumerate(((sum_ref, CROSS), (cross_ref, 0))):
+            owner = core if own == 0 else 1 - core
+            for k in range(3):
+                for j in range(SLABS):
+                    high, low = split(gref[pl.ds(base + (k * SLABS + j) * F, F), :])
+                    cols = slice(j * LANES, (j + 1) * LANES)
+                    gh[3 * owner + k, :, cols] = high
+                    gl[3 * owner + k, :, cols] = low
+
     where = {(1, 0): 0, (2, 0): 1, (3, 1): 2, (3, 2): 3, (2, 1): 4, (3, 0): 5}
-
-    def one(half, _):
-        cols = pl.ds(pl.multiple_of(half * 256, 256), 256)
-        rounded = []
-        for b in range(4):
-            corr = jnp.concatenate(
-                [
-                    sum_ref[pl.ds(pl.multiple_of(MOMENT + (b * SLABS + 2 * half + k) * F, F), F), :]
-                    for k in range(2)
-                ],
-                axis=1,
-            )
-            for j in range(b):
-                corr = corr - (dot(gh[where[b, j]], rounded[j]) + dot(gl[where[b, j]], rounded[j]))
-            ch, cl = split(corr)
-            delta = dot(ih[b], ch) + (dot(ih[b], cl) + dot(il[b], ch))
-            coef_ref[b, :, cols] = delta
-            rounded.append(delta.astype(jnp.bfloat16))
-        fit = lax.dot_general(
-            ft_ref[0], rounded[0], (((0,), (0,)), ((), ())), preferred_element_type=jnp.float32
+    rounded = []
+    for b in range(4):
+        corr = jnp.concatenate(
+            [
+                sum_ref[pl.ds(pl.multiple_of(MOMENT + (b * SLABS + 2 * half + k) * F, F), F), :]
+                for k in range(2)
+            ],
+            axis=1,
         )
-        for b in range(1, 4):
-            fit = fit + lax.dot_general(
-                ft_ref[b], rounded[b], (((0,), (0,)), ((), ())), preferred_element_type=jnp.float32
-            )
-        res_ref[:, cols] = y_ref[:, cols].astype(jnp.float32) - fit
-        return 0
-
-    lax.fori_loop(0, 2, one, 0)
+        for j in range(b):
+            corr = corr - (dot(gh[where[b, j]], rounded[j]) + dot(gl[where[b, j]], rounded[j]))
+        ch, cl = split(corr)
+        delta = dot(ih[b], ch) + (dot(ih[b], cl) + dot(il[b], ch))
+        coef_ref[b] = delta
+        rounded.append(delta.astype(jnp.bfloat16))
+    fit = lax.dot_general(
+        ft_ref[0], rounded[0], (((0,), (0,)), ((), ())), preferred_element_type=jnp.float32
+    )
+    for b in range(1, 4):
+        fit = fit + lax.dot_general(
+            ft_ref[b], rounded[b], (((0,), (0,)), ((), ())), preferred_element_type=jnp.float32
+        )
+    res_ref[...] = y_ref[...].astype(jnp.float32) - fit
 
 
 def sweep(summed, cross, high, low, ft, y):
-    vmem = pl.BlockSpec(memory_space=pltpu.VMEM)
+    rows, cols = y.shape
+
+    def whole(array):
+        return pl.BlockSpec(array.shape, lambda i: (0,) * array.ndim, pipeline_mode=pl.Buffered(1))
+
     return pl.pallas_call(
         sweep_kernel,
+        grid=(2,),
         out_shape=(
-            jax.ShapeDtypeStruct((4, F, y.shape[1]), jnp.float32),
+            jax.ShapeDtypeStruct((4, F, cols), jnp.float32),
             jax.ShapeDtypeStruct(y.shape, jnp.float32),
         ),
-        in_specs=[vmem] * 6,
-        out_specs=(vmem, vmem),
+        in_specs=[whole(v) for v in (summed, cross, high, low, ft)]
+        + [pl.BlockSpec((rows, cols // 2), lambda i: (0, i))],
+        out_specs=(
+            pl.BlockSpec((4, F, cols // 2), lambda i: (0, 0, i)),
+            pl.BlockSpec((rows, cols // 2), lambda i: (0, i)),
+        ),
         scratch_shapes=[pltpu.VMEM((6, F, F), jnp.bfloat16), pltpu.VMEM((6, F, F), jnp.bfloat16)],
         compiler_params=pltpu.CompilerParams(vmem_limit_bytes=60 * 2**20),
         name="sweep",

time: 162 us -> 156 us (0.963)
  Pallas kernels: 161 us -> 155 us
    pallas_call x1, Pallas kernels: 138 us -> 134 us  [sum_and_invert(): pl.pallas_call(functools.partial(sum_kernel, plan, scale), out_shape=(jax...]
where the time goes in v5:
time: 156 us
  Pallas kernels  155 us (99%)
    pallas_call x1, Pallas kernels, sum_and_invert(): pl.pallas_call(functools.partial(sum_kernel, plan, scale), out_shape=(jax...  134 us
    pallas_call x1, Pallas kernels, sweep(): pl.pallas_call(sweep_kernel, grid=(2,), out_shape=(jax.ShapeDtypeStruct((...  21.9 us

profile of v5, /device:TPU:1, one launch (start us, length us, event | category | flops | bytes accessed | tf_op | source)
XLA Modules:
  0.0 156.0 jit_solution(7200695446945883093)
XLA Ops:
  0.6 133.5 %sum_and_invert.1 = (bf16[4,512,1024]{2,1,0:T(8,128)(2,1)}, f32[16896,128]{1,0:T(8,128)}, f32[6144,128]{1,0:T(8,128)}, bf16[4,512,512]{2,1,0:T(8,128)(2,1)}, bf16[4,512,512]{2,1,0:T(8,128)(2,1)}) custom-call(bf16[440,1024]{1,0:T(8,128)(2,1)} %bitcast.1, bf16[2,440,512]{2,1,0:T(8,128)(2,1)} %proj_ref.1, bf16[2,512]{1,0:T(2,128)(2,1)} %phase_ref.1, ...), custom_call_target="tpu_custom_call" | custom-call | tf_op jit(solution)/shard_map/sum_and_invert/pallas_call | solution.py:605
  134.2 21.9 %sweep.1 = (f32[4,512,512]{2,1,0:T(8,128)}, f32[1024,512]{1,0:T(8,128)}) custom-call(f32[16896,128]{1,0:T(8,128)} %get-tuple-element.7.sum_ref, f32[6144,128]{1,0:T(8,128)} %get-tuple-element.8.cross_ref, bf16[4,512,512]{2,1,0:T(8,128)(2,1)} %get-tuple-element.9.ih, bf16[4,512,512]{2,1,0:T(8,128)(2,1)} %get-tuple-element.10.il, ...), custom_call_target="tpu_custom_call" | custom-call | tf_op jit(solution)/shard_map/sweep/pallas_call | solution.py:691
